TPU v7x, 32 devices: a whole 2x2x4 slice. The times are simulated.
32 devices in a mesh: shard: 2 (over x), ctx: 4 (over z), tp: 4 (over y, core).
Axes of the slice: x: 2, y: 2, z: 4, core: 2. Of those that a mesh axis runs over, the one named last changes fastest.
Arguments:
- tokens: bfloat16 [4, 1024, 768], P('shard', ('ctx', 'tp')), may hold values from -6 to 6
- cotangent: bfloat16 [4, 1024, 768], P('shard', ('ctx', 'tp')), may hold values from -6 to 6
- segment_ids: int32 [4, 1024], P('shard'), may hold values from 0 to 7, never falling along the last dimension, each value on 1 to 512 neighbouring positions
- lengths: int32 [4], P('shard'), may hold values from 768 to 1024
- query_weight: bfloat16 [2, 768, 768], P(None, 'shard', 'tp'), may hold values from -0.21875 to 0.21875
- key_weight: bfloat16 [2, 768, 768], P(None, 'shard', 'tp'), may hold values from -0.21875 to 0.21875
- value_weight: bfloat16 [2, 768, 768], P(None, 'shard', 'tp'), may hold values from -0.21875 to 0.21875
- output_weight: bfloat16 [2, 768, 768], P(None, 'tp', 'shard'), may hold values from -1.75 to 1.75
- inner_weight: bfloat16 [2, 768, 3072], P(None, 'shard', 'tp'), may hold values from -0.21875 to 0.21875
- outer_weight: bfloat16 [2, 3072, 768], P(None, 'tp', 'shard'), may hold values from -0.109375 to 0.109375
- query_bias: bfloat16 [2, 768], P(None, 'shard'), may hold values from -3 to 3
- value_bias: bfloat16 [2, 768], P(None, 'shard'), may hold values from -0.29882812 to 0.29882812
- output_bias: bfloat16 [2, 768], P(None, 'shard'), may hold values from -0.59765625 to 0.59765625
- inner_bias: bfloat16 [2, 3072], P(None, 'shard'), may hold values from -1.1953125 to 1.1953125
- outer_bias: bfloat16 [2, 768], P(None, 'shard'), may hold values from -0.59765625 to 0.59765625
- first_gain: bfloat16 [2, 768], P(None, 'shard'), may hold values from 0.5 to 1.5
- first_shift: bfloat16 [2, 768], P(None, 'shard'), may hold values from -0.59765625 to 0.59765625
- second_gain: bfloat16 [2, 768], P(None, 'shard'), may hold values from 0.5 to 1.5
- second_shift: bfloat16 [2, 768], P(None, 'shard'), may hold values from -0.59765625 to 0.59765625
Outputs:
- layer_out: bfloat16 [4, 1024, 768], P('shard', ('ctx', 'tp'))
- grad_tokens: float32 [4, 1024, 768], P('shard', ('ctx', 'tp'))
- grad_query_weight: float32 [2, 768, 768], P(None, 'shard', 'tp')
- grad_key_weight: float32 [2, 768, 768], P(None, 'shard', 'tp')
- grad_value_weight: float32 [2, 768, 768], P(None, 'shard', 'tp')
- grad_output_weight: float32 [2, 768, 768], P(None, 'tp', 'shard')
- grad_inner_weight: float32 [2, 768, 3072], P(None, 'shard', 'tp')
- grad_outer_weight: float32 [2, 3072, 768], P(None, 'tp', 'shard')
- grad_query_bias: float32 [2, 768], P(None, 'shard')
- grad_value_bias: float32 [2, 768], P(None, 'shard')
- grad_output_bias: float32 [2, 768], P(None, 'shard')
- grad_inner_bias: float32 [2, 3072], P(None, 'shard')
- grad_outer_bias: float32 [2, 768], P(None, 'shard')
- grad_first_gain: float32 [2, 768], P(None, 'shard')
- grad_first_shift: float32 [2, 768], P(None, 'shard')
- grad_second_gain: float32 [2, 768], P(None, 'shard')
- grad_second_shift: float32 [2, 768], P(None, 'shard')
Inputs may be any that keep to these rules, and one draw needn't show every extreme that they name: `segment_ids`: along each sequence the document numbers never fall, and no document has more than 512 positions. `lengths`: positions at or past a sequence's length are padding.
All inputs are finite; a program needn't handle non-finite values.
Results may differ from a plain program's by a relative error of at most 0.04.
Values may be sent and summed in bfloat16 or wider, within the bound.
A program may use at most 128 MiB of HBM per device.

v0:
```python
import jax
import jax.numpy as jnp
from jax import lax
from jax.sharding import PartitionSpec as P

HD = 64
LAYERS = 2


EPSILON = 1e-05


def layer_norm(resid, gain, shift):
    center = resid - jnp.mean(resid, axis=-1, keepdims=True)
    spread = jnp.mean(center * center, axis=-1, keepdims=True)
    return center * lax.rsqrt(spread + EPSILON) * gain + shift


def gelu_exact(pre_act):
    return jax.nn.gelu(pre_act, approximate=False)


def rows_all(local_rows):
    return lax.all_gather(local_rows, "tp", axis=1, tiled=True)


def rows_sum(partial_rows):
    return lax.psum_scatter(
        partial_rows.astype(jnp.bfloat16), "tp", scatter_dimension=1, tiled=True
    ).astype(jnp.float32)


def fetch(layer_at, params):
    (
        query_weight,
        key_weight,
        value_weight,
        output_weight,
        inner_weight,
        outer_weight,
        query_bias,
        value_bias,
        output_bias,
        inner_bias,
        outer_bias,
        first_gain,
        first_shift,
        second_gain,
        second_shift,
    ) = params
    return (
        lax.all_gather(query_weight[layer_at], "shard", axis=0, tiled=True),
        lax.all_gather(key_weight[layer_at], "shard", axis=0, tiled=True),
        lax.all_gather(value_weight[layer_at], "shard", axis=0, tiled=True),
        lax.all_gather(output_weight[layer_at], "shard", axis=1, tiled=True),
        lax.all_gather(inner_weight[layer_at], "shard", axis=0, tiled=True),
        lax.all_gather(outer_weight[layer_at], "shard", axis=1, tiled=True),
        lax.all_gather(query_bias[layer_at], "shard", axis=0, tiled=True),
        lax.all_gather(value_bias[layer_at], "shard", axis=0, tiled=True),
        lax.all_gather(output_bias[layer_at], "shard", axis=0, tiled=True),
        lax.all_gather(inner_bias[layer_at], "shard", axis=0, tiled=True),
        lax.all_gather(outer_bias[layer_at], "shard", axis=0, tiled=True),
        lax.all_gather(first_gain[layer_at], "shard", axis=0, tiled=True),
        lax.all_gather(first_shift[layer_at], "shard", axis=0, tiled=True),
        lax.all_gather(second_gain[layer_at], "shard", axis=0, tiled=True),
        lax.all_gather(second_shift[layer_at], "shard", axis=0, tiled=True),
    )


def column_slice(vector, start, count):
    return lax.dynamic_slice_in_dim(vector, start, count).astype(jnp.float32)


def placed(piece, start, total):
    return lax.dynamic_update_slice(jnp.zeros((total,), jnp.float32), piece, (start,))


def attention_probs(query_four, key_four, query_ids, key_ids):
    scores = jnp.einsum(
        "sqhd,skhd->shqk", query_four, key_four, preferred_element_type=jnp.float32
    ) * HD ** (-0.5)
    allowed = query_ids[:, None, :, None] == key_ids[:, None, None, :]
    scores = jnp.where(allowed, scores, -1e30)
    row_top = jnp.max(scores, axis=-1, keepdims=True)
    expo = jnp.exp(scores - row_top)
    return expo / jnp.sum(expo, axis=-1, keepdims=True)


def layer_forward(resid_in, weights, query_ids, key_ids, offsets):
    (
        query_weight,
        key_weight,
        value_weight,
        output_weight,
        inner_weight,
        outer_weight,
        query_bias,
        value_bias,
        output_bias,
        inner_bias,
        outer_bias,
        first_gain,
        first_shift,
        second_gain,
        second_shift,
    ) = weights
    col_start, unit_start = offsets
    col_count = query_weight.shape[1]
    unit_count = inner_weight.shape[1]
    seq_count = resid_in.shape[0]
    head_count = col_count // HD
    rows_in = rows_all(resid_in.astype(jnp.bfloat16))
    block_len = rows_in.shape[1]
    query_rows = (
        jnp.dot(rows_in, query_weight, preferred_element_type=jnp.float32)
        + column_slice(query_bias, col_start, col_count)
    ).astype(jnp.bfloat16)
    key_rows = jnp.dot(rows_in, key_weight, preferred_element_type=jnp.float32).astype(jnp.bfloat16)
    value_rows = (
        jnp.dot(rows_in, value_weight, preferred_element_type=jnp.float32)
        + column_slice(value_bias, col_start, col_count)
    ).astype(jnp.bfloat16)
    key_full, value_full = (
        lax.all_gather(key_rows, "ctx", axis=1, tiled=True),
        lax.all_gather(value_rows, "ctx", axis=1, tiled=True),
    )
    full_len = key_full.shape[1]
    query_four = query_rows.reshape(seq_count, block_len, head_count, HD)
    key_four = key_full.reshape(seq_count, full_len, head_count, HD)
    value_four = value_full.reshape(seq_count, full_len, head_count, HD)
    attn_probs = attention_probs(query_four, key_four, query_ids, key_ids)
    probs_low = attn_probs.astype(jnp.bfloat16)
    mixed_low = (
        jnp.einsum("shqk,skhd->sqhd", probs_low, value_four, preferred_element_type=jnp.float32)
        .reshape(seq_count, block_len, col_count)
        .astype(jnp.bfloat16)
    )
    branch = rows_sum(
        jnp.dot(mixed_low, output_weight, preferred_element_type=jnp.float32)
    ) + output_bias.astype(jnp.float32)
    first_sum = resid_in + branch
    normed = layer_norm(first_sum, first_gain.astype(jnp.float32), first_shift.astype(jnp.float32))
    normed_rows = rows_all(normed.astype(jnp.bfloat16))
    inner_pre = jnp.dot(
        normed_rows, inner_weight, preferred_element_type=jnp.float32
    ) + column_slice(inner_bias, unit_start, unit_count)
    active = gelu_exact(inner_pre).astype(jnp.bfloat16)
    outer_sum = rows_sum(
        jnp.dot(active, outer_weight, preferred_element_type=jnp.float32)
    ) + outer_bias.astype(jnp.float32)
    second = normed + outer_sum
    result = layer_norm(second, second_gain.astype(jnp.float32), second_shift.astype(jnp.float32))
    saved = (
        rows_in,
        query_four,
        key_four,
        value_four,
        attn_probs,
        probs_low,
        mixed_low,
        first_sum,
        normed_rows,
        inner_pre,
        active,
        second,
    )
    return (result, saved)


def layer_backward(grad_out, weights, saved, offsets):
    (
        query_weight,
        key_weight,
        value_weight,
        output_weight,
        inner_weight,
        outer_weight,
        query_bias,
        value_bias,
        output_bias,
        inner_bias,
        outer_bias,
        first_gain,
        first_shift,
        second_gain,
        second_shift,
    ) = weights
    (
        rows_in,
        query_four,
        key_four,
        value_four,
        attn_probs,
        probs_low,
        mixed_low,
        first_sum,
        normed_rows,
        inner_pre,
        active,
        second,
    ) = saved
    col_start, unit_start = offsets
    seq_count, block_len, col_count = mixed_low.shape
    full_len = key_four.shape[1]
    scale = HD ** (-0.5)
    _, second_pull = jax.vjp(
        layer_norm, second, second_gain.astype(jnp.float32), second_shift.astype(jnp.float32)
    )
    grad_second, grad_second_gain, grad_second_shift = second_pull(grad_out)
    grad_outer = grad_second.astype(jnp.bfloat16)
    grad_outer_bias = jnp.sum(grad_outer.astype(jnp.float32), axis=(0, 1))
    outer_rows = rows_all(grad_outer)
    grad_outer_weight = jnp.einsum(
        "sri,srj->ij", active, outer_rows, preferred_element_type=jnp.float32
    )
    grad_active = jnp.einsum(
        "srj,ij->sri", outer_rows, outer_weight, preferred_element_type=jnp.float32
    )
    _, gelu_pull = jax.vjp(gelu_exact, inner_pre)
    grad_inner = gelu_pull(grad_active)[0].astype(jnp.bfloat16)
    grad_inner_bias = jnp.sum(grad_inner.astype(jnp.float32), axis=(0, 1))
    grad_inner_weight = jnp.einsum(
        "sri,srj->ij", normed_rows, grad_inner, preferred_element_type=jnp.float32
    )
    grad_normed = grad_second + rows_sum(
        jnp.einsum("srj,ij->sri", grad_inner, inner_weight, preferred_element_type=jnp.float32)
    )
    _, first_pull = jax.vjp(
        layer_norm, first_sum, first_gain.astype(jnp.float32), first_shift.astype(jnp.float32)
    )
    grad_first, grad_first_gain, grad_first_shift = first_pull(grad_normed)
    grad_branch = grad_first.astype(jnp.bfloat16)
    grad_output_bias = jnp.sum(grad_branch.astype(jnp.float32), axis=(0, 1))
    branch_rows = rows_all(grad_branch)
    grad_output_weight = jnp.einsum(
        "sri,srj->ij", mixed_low, branch_rows, preferred_element_type=jnp.float32
    )
    grad_mixed = jnp.einsum(
        "srj,ij->sri", branch_rows, output_weight, preferred_element_type=jnp.float32
    )
    grad_mixed = grad_mixed.astype(jnp.bfloat16).reshape(query_four.shape)
    grad_probs = jnp.einsum(
        "sqhd,skhd->shqk", grad_mixed, value_four, preferred_element_type=jnp.float32
    )
    inner_total = jnp.sum(attn_probs * grad_probs, axis=-1, keepdims=True)
    grad_scores = (attn_probs * (grad_probs - inner_total)).astype(jnp.bfloat16)
    grad_query = (
        jnp.einsum("shqk,skhd->sqhd", grad_scores, key_four, preferred_element_type=jnp.float32)
        * scale
    )
    grad_query = grad_query.astype(jnp.bfloat16).reshape(seq_count, block_len, col_count)
    key_term = (
        jnp.einsum("shqk,sqhd->skhd", grad_scores, query_four, preferred_element_type=jnp.float32)
        * scale
    ).reshape(seq_count, full_len, col_count)
    value_term = jnp.einsum(
        "shqk,sqhd->skhd", probs_low, grad_mixed, preferred_element_type=jnp.float32
    ).reshape(seq_count, full_len, col_count)
    grad_keys, grad_values = (
        lax.psum_scatter(
            key_term.astype(jnp.bfloat16), "ctx", scatter_dimension=1, tiled=True
        ).astype(jnp.float32),
        lax.psum_scatter(
            value_term.astype(jnp.bfloat16), "ctx", scatter_dimension=1, tiled=True
        ).astype(jnp.float32),
    )
    grad_keys = grad_keys.astype(jnp.bfloat16)
    grad_values = grad_values.astype(jnp.bfloat16)
    grad_query_weight = jnp.einsum(
        "sri,srj->ij", rows_in, grad_query, preferred_element_type=jnp.float32
    )
    grad_key_weight = jnp.einsum(
        "sri,srj->ij", rows_in, grad_keys, preferred_element_type=jnp.float32
    )
    grad_value_weight = jnp.einsum(
        "sri,srj->ij", rows_in, grad_values, preferred_element_type=jnp.float32
    )
    back_rows = (
        jnp.einsum("srj,ij->sri", grad_query, query_weight, preferred_element_type=jnp.float32)
        + jnp.einsum("srj,ij->sri", grad_keys, key_weight, preferred_element_type=jnp.float32)
        + jnp.einsum("srj,ij->sri", grad_values, value_weight, preferred_element_type=jnp.float32)
    )
    grad_input = grad_first + rows_sum(back_rows)
    model_width = query_bias.shape[0]
    grad_query_bias = placed(
        jnp.sum(grad_query.astype(jnp.float32), axis=(0, 1)), col_start, model_width
    )
    grad_value_bias = placed(
        jnp.sum(grad_values.astype(jnp.float32), axis=(0, 1)), col_start, model_width
    )
    grad_inner_full = placed(grad_inner_bias, unit_start, inner_bias.shape[0])
    matrices = (
        grad_query_weight,
        grad_key_weight,
        grad_value_weight,
        grad_output_weight,
        grad_inner_weight,
        grad_outer_weight,
    )
    vectors = (
        grad_query_bias,
        grad_value_bias,
        grad_output_bias,
        grad_inner_full,
        grad_outer_bias,
        grad_first_gain,
        grad_first_shift,
        grad_second_gain,
        grad_second_shift,
    )
    return (grad_input, matrices, vectors)


def reduce_grads(matrices, vectors):
    mat_query, mat_key, mat_value, mat_output, mat_inner, mat_outer = matrices
    (
        vec_query,
        vec_value,
        vec_output,
        vec_inner,
        vec_outer,
        vec_gain_one,
        vec_shift_one,
        vec_gain_two,
        vec_shift_two,
    ) = vectors
    part_query, part_key, part_value, part_output, part_inner, part_outer = (
        lax.psum_scatter(
            mat_query.astype(jnp.bfloat16), "shard", scatter_dimension=0, tiled=True
        ).astype(jnp.float32),
        lax.psum_scatter(
            mat_key.astype(jnp.bfloat16), "shard", scatter_dimension=0, tiled=True
        ).astype(jnp.float32),
        lax.psum_scatter(
            mat_value.astype(jnp.bfloat16), "shard", scatter_dimension=0, tiled=True
        ).astype(jnp.float32),
        lax.psum_scatter(
            mat_output.astype(jnp.bfloat16), "shard", scatter_dimension=1, tiled=True
        ).astype(jnp.float32),
        lax.psum_scatter(
            mat_inner.astype(jnp.bfloat16), "shard", scatter_dimension=0, tiled=True
        ).astype(jnp.float32),
        lax.psum_scatter(
            mat_outer.astype(jnp.bfloat16), "shard", scatter_dimension=1, tiled=True
        ).astype(jnp.float32),
    )
    summed = (
        lax.psum(part_query.astype(jnp.bfloat16), "ctx").astype(jnp.float32),
        lax.psum(part_key.astype(jnp.bfloat16), "ctx").astype(jnp.float32),
        lax.psum(part_value.astype(jnp.bfloat16), "ctx").astype(jnp.float32),
        lax.psum(part_output.astype(jnp.bfloat16), "ctx").astype(jnp.float32),
        lax.psum(part_inner.astype(jnp.bfloat16), "ctx").astype(jnp.float32),
        lax.psum(part_outer.astype(jnp.bfloat16), "ctx").astype(jnp.float32),
    )
    vec_sums = lax.psum(
        (
            vec_query,
            vec_value,
            vec_output,
            vec_inner,
            vec_outer,
            vec_gain_one,
            vec_shift_one,
            vec_gain_two,
            vec_shift_two,
        ),
        ("shard", "ctx", "tp"),
    )
    shard_count = lax.axis_size("shard")
    shard_at = lax.axis_index("shard")
    owned = tuple(
        (
            lax.dynamic_slice_in_dim(
                vec_item,
                shard_at * (vec_item.shape[0] // shard_count),
                vec_item.shape[0] // shard_count,
            )
            for vec_item in vec_sums
        )
    )
    return (tuple(summed), owned)


def per_device(
    tokens,
    cotangent,
    segment_ids,
    lengths,
    query_weight,
    key_weight,
    value_weight,
    output_weight,
    inner_weight,
    outer_weight,
    query_bias,
    value_bias,
    output_bias,
    inner_bias,
    outer_bias,
    first_gain,
    first_shift,
    second_gain,
    second_shift,
):
    params = (
        query_weight,
        key_weight,
        value_weight,
        output_weight,
        inner_weight,
        outer_weight,
        query_bias,
        value_bias,
        output_bias,
        inner_bias,
        outer_bias,
        first_gain,
        first_shift,
        second_gain,
        second_shift,
    )
    ctx_index = lax.axis_index("ctx")
    tp_index = lax.axis_index("tp")
    offsets = (tp_index * query_weight.shape[2], tp_index * inner_weight.shape[2])
    positions = lax.broadcasted_iota(jnp.int32, segment_ids.shape, 1)
    key_ids = jnp.where(positions < lengths[:, None], segment_ids, -1)
    block_len = segment_ids.shape[1] // lax.axis_size("ctx")
    query_ids = lax.dynamic_slice_in_dim(key_ids, ctx_index * block_len, block_len, 1)
    resid = tokens.astype(jnp.float32)
    layer_inputs = []
    fetched = []
    for layer_at in range(LAYERS):
        weights = fetch(layer_at, params)
        fetched.append(weights)
        layer_inputs.append(resid)
        resid, _ = layer_forward(resid, weights, query_ids, key_ids, offsets)
    layer_out = resid.astype(jnp.bfloat16)
    grad_flow = cotangent.astype(jnp.float32)
    mat_grads = [None] * LAYERS
    vec_grads = [None] * LAYERS
    for layer_at in reversed(range(LAYERS)):
        weights = fetch(layer_at, params)
        _, saved = layer_forward(layer_inputs[layer_at], weights, query_ids, key_ids, offsets)
        grad_flow, matrices, vectors = layer_backward(grad_flow, weights, saved, offsets)
        mat_grads[layer_at], vec_grads[layer_at] = reduce_grads(matrices, vectors)
    stacked_mats = tuple(
        (
            jnp.stack([mat_grads[layer_at][item_at] for layer_at in range(LAYERS)])
            for item_at in range(6)
        )
    )
    stacked_vecs = tuple(
        (
            jnp.stack([vec_grads[layer_at][item_at] for layer_at in range(LAYERS)])
            for item_at in range(9)
        )
    )
    return (layer_out, grad_flow) + stacked_mats + stacked_vecs


def solution(mesh):
    return jax.shard_map(
        per_device,
        mesh=mesh,
        in_specs=(
            P("shard", ("ctx", "tp"), None),
            P("shard", ("ctx", "tp"), None),
            P("shard", None),
            P("shard"),
            P(None, "shard", "tp"),
            P(None, "shard", "tp"),
            P(None, "shard", "tp"),
            P(None, "tp", "shard"),
            P(None, "shard", "tp"),
            P(None, "tp", "shard"),
            P(None, "shard"),
            P(None, "shard"),
            P(None, "shard"),
            P(None, "shard"),
            P(None, "shard"),
            P(None, "shard"),
            P(None, "shard"),
            P(None, "shard"),
            P(None, "shard"),
        ),
        out_specs=(
            P("shard", ("ctx", "tp"), None),
            P("shard", ("ctx", "tp"), None),
            P(None, "shard", "tp"),
            P(None, "shard", "tp"),
            P(None, "shard", "tp"),
            P(None, "tp", "shard"),
            P(None, "shard", "tp"),
            P(None, "tp", "shard"),
            P(None, "shard"),
            P(None, "shard"),
            P(None, "shard"),
            P(None, "shard"),
            P(None, "shard"),
            P(None, "shard"),
            P(None, "shard"),
            P(None, "shard"),
            P(None, "shard"),
        ),
        check_vma=False,
    )
```

profile of v0, /device:TPU:0, one launch (start us, length us, event | category | flops | bytes accessed | tf_op | source)
XLA Modules:
  0.0 958.1 jit_solution(9860618965255192818)
XLA Ops:
  8.9 5.3 all-gather.3
  20.4 5.8 all-gather.2
  27.4 7.1 all-gather.4
  34.6 7.1 all-gather
  41.7 5.8 all-gather.5
  48.8 8.9 all_gather.162
  58.1 19.8 %all_gather.169 = bf16[2,1024,192]{1,2,0:T(8,128)(2,1)S(1)} all-gather(bf16[2,256,192]{1,2,0:T(8,128)(2,1)S(1)} %convolution_convert_fusion.9), channel_id=1, replica_groups=mesh['shard'=2,'ctx'=4,'tp'=4] {'ctx'}, dimensions={1}, use_global_device_ids=true | all-gather | bytes 983040 | tf_op jit(solution)/shard_map/all_gather | solution.py:124
  78.3 18.0 %all_gather.165 = bf16[2,1024,192]{1,2,0:T(8,128)(2,1)S(1)} all-gather(bf16[2,256,192]{1,2,0:T(8,128)(2,1)S(1)} %fusion.54), channel_id=1, replica_groups=mesh['shard'=2,'ctx'=4,'tp'=4] {'ctx'}, dimensions={1}, use_global_device_ids=true | all-gather | bytes 983040 | tf_op jit(solution)/shard_map/all_gather | solution.py:125
  96.8 6.2 fusion.143
  127.6 4.6 all-gather.10
  135.6 7.5 all_gather.174
  151.4 6.0 all-gather.37.cloned.1.call-done
  184.0 5.8 all-gather.17
  189.8 5.8 all-gather.19
  195.6 6.3 all-gather.15
  201.9 5.8 all-gather.20
  209.5 8.6 all_gather.181
  218.5 19.7 %all_gather.188 = bf16[2,1024,192]{1,2,0:T(8,128)(2,1)S(1)} all-gather(bf16[2,256,192]{1,2,0:T(8,128)(2,1)S(1)} %convolution_convert_fusion.8), channel_id=1, replica_groups=mesh['shard'=2,'ctx'=4,'tp'=4] {'ctx'}, dimensions={1}, use_global_device_ids=true | all-gather | bytes 983040 | tf_op jit(solution)/shard_map/all_gather | solution.py:124
  238.6 18.1 %all_gather.184 = bf16[2,1024,192]{1,2,0:T(8,128)(2,1)S(1)} all-gather(bf16[2,256,192]{1,2,0:T(8,128)(2,1)S(1)} %fusion.56), channel_id=1, replica_groups=mesh['shard'=2,'ctx'=4,'tp'=4] {'ctx'}, dimensions={1}, use_global_device_ids=true | all-gather | bytes 983040 | tf_op jit(solution)/shard_map/all_gather | solution.py:125
  257.2 5.1 fusion.144
  282.3 4.6 all-gather.25
  289.9 8.5 all_gather.193
  301.2 4.6 multiply_convert_fusion.4
  305.9 9.3 all-gather.41.cloned.1.call-done
  331.6 10.2 %reduce-scatter.51.cloned.1.call-done = bf16[2,64,768]{2,1,0:T(8,128)(2,1)} async-done(((bf16[2,256,768]{2,1,0:T(8,128)(2,1)}), bf16[2,64,768]{2,1,0:T(8,128)(2,1)}) %reduce-scatter.51.cloned.1.call-update) | async-done | bytes 196624 | tf_op jit(solution)/shard_map/reduce_scatter | solution.py:28
  345.6 8.2 all_gather.200
  358.3 23.9 %reduce-scatter.53.cloned.1.call-done = bf16[2,64,768]{2,1,0:T(8,128)(2,1)} async-done(((bf16[2,256,768]{2,1,0:T(8,128)(2,1)}), bf16[2,64,768]{2,1,0:T(8,128)(2,1)}) %reduce-scatter.53.cloned.1.call-update) | async-done | bytes 196624 | tf_op jit(solution)/shard_map/reduce_scatter | solution.py:28
  386.0 8.0 all_gather.201
  412.2 15.2 %reduce-scatter.55.cloned.1.call-done = bf16[2,256,192]{1,2,0:T(8,128)(2,1)} async-done(((bf16[2,1024,192]{1,2,0:T(8,128)(2,1)}), bf16[2,256,192]{1,2,0:T(8,128)(2,1)}) %reduce-scatter.55.cloned.1.call-update) | async-done | bytes 196624 | tf_op jit(solution)/shard_map/reduce_scatter | solution.py:260
  428.8 23.5 %reduce-scatter.57.cloned.1.call-done = bf16[2,256,192]{1,2,0:T(8,128)(2,1)} async-done(((bf16[2,1024,192]{1,2,0:T(8,128)(2,1)}), bf16[2,256,192]{1,2,0:T(8,128)(2,1)}) %reduce-scatter.57.cloned.1.call-update) | async-done | bytes 196624 | tf_op jit(solution)/shard_map/reduce_scatter | solution.py:263
  454.8 22.7 %reduce-scatter.59.cloned.1.call-done = bf16[2,64,768]{2,1,0:T(8,128)(2,1)} async-done(((bf16[2,256,768]{2,1,0:T(8,128)(2,1)}), bf16[2,64,768]{2,1,0:T(8,128)(2,1)}) %reduce-scatter.59.cloned.1.call-update) | async-done | bytes 196624 | tf_op jit(solution)/shard_map/reduce_scatter | solution.py:28
  481.7 8.0 all_gather.202
  494.2 23.9 %reduce-scatter.61.cloned.1.call-done = bf16[2,64,768]{2,1,0:T(8,128)(2,1)} async-done(((bf16[2,256,768]{2,1,0:T(8,128)(2,1)}), bf16[2,64,768]{2,1,0:T(8,128)(2,1)}) %reduce-scatter.61.cloned.1.call-update) | async-done | bytes 196624 | tf_op jit(solution)/shard_map/reduce_scatter | solution.py:28
  521.9 8.0 all_gather.203
  531.3 4.6 fusion.30
  602.2 14.3 %reduce-scatter.75.cloned.1.call-done = bf16[384,192]{1,0:T(8,128)(2,1)} async-done(((bf16[768,192]{1,0:T(8,128)(2,1)}), bf16[384,192]{1,0:T(8,128)(2,1)}) %reduce-scatter.75.cloned.1.call-update) | async-done | bytes 147472
  618.2 22.3 %reduce-scatter.91.cloned.1.call-done = bf16[384,768]{1,0:T(8,128)(2,1)} async-done(((bf16[768,768]{1,0:T(8,128)(2,1)}), bf16[384,768]{1,0:T(8,128)(2,1)}) %reduce-scatter.91.cloned.1.call-update) | async-done | bytes 589840
  642.6 13.3 %reduce-scatter.83.cloned.1.call-done = bf16[384,192]{1,0:T(8,128)(2,1)} async-done(((bf16[768,192]{1,0:T(8,128)(2,1)}), bf16[384,192]{1,0:T(8,128)(2,1)}) %reduce-scatter.83.cloned.1.call-update) | async-done | bytes 147472
  657.6 14.1 %reduce-scatter.79.cloned.1.call-done = bf16[384,192]{1,0:T(8,128)(2,1)} async-done(((bf16[768,192]{1,0:T(8,128)(2,1)}), bf16[384,192]{1,0:T(8,128)(2,1)}) %reduce-scatter.79.cloned.1.call-update) | async-done | bytes 147472
  673.5 13.7 %reduce-scatter.85.cloned.1.call-done = bf16[384,192]{1,0:T(8,128)(2,1)} async-done(((bf16[768,192]{1,0:T(8,128)(2,1)}), bf16[384,192]{1,0:T(8,128)(2,1)}) %reduce-scatter.85.cloned.1.call-update) | async-done | bytes 147472
  688.9 14.3 %reduce-scatter.73.cloned.1.call-done = bf16[384,192]{1,0:T(8,128)(2,1)} async-done(((bf16[768,192]{1,0:T(8,128)(2,1)}), bf16[384,192]{1,0:T(8,128)(2,1)}) %reduce-scatter.73.cloned.1.call-update) | async-done | bytes 147472
  704.9 22.4 %reduce-scatter.89.cloned.1.call-done = bf16[384,768]{1,0:T(8,128)(2,1)} async-done(((bf16[768,768]{1,0:T(8,128)(2,1)}), bf16[384,768]{1,0:T(8,128)(2,1)}) %reduce-scatter.89.cloned.1.call-update) | async-done | bytes 589840
  729.4 13.3 %reduce-scatter.81.cloned.1.call-done = bf16[384,192]{1,0:T(8,128)(2,1)} async-done(((bf16[768,192]{1,0:T(8,128)(2,1)}), bf16[384,192]{1,0:T(8,128)(2,1)}) %reduce-scatter.81.cloned.1.call-update) | async-done | bytes 147472
  744.4 14.3 %reduce-scatter.77.cloned.1.call-done = bf16[384,192]{1,0:T(8,128)(2,1)} async-done(((bf16[768,192]{1,0:T(8,128)(2,1)}), bf16[384,192]{1,0:T(8,128)(2,1)}) %reduce-scatter.77.cloned.1.call-update) | async-done | bytes 147472
  760.5 22.8 %reduce-scatter.71.cloned.1.call-done = bf16[384,768]{1,0:T(8,128)(2,1)} async-done(((bf16[768,768]{1,0:T(8,128)(2,1)}), bf16[384,768]{1,0:T(8,128)(2,1)}) %reduce-scatter.71.cloned.1.call-update) | async-done | bytes 589840 | tf_op jit(solution)/shard_map/reduce_scatter | solution.py:340
  783.2 24.6 %reduce-scatter.69.cloned.1.call-done = bf16[384,768]{1,0:T(8,128)(2,1)} async-done(((bf16[768,768]{1,0:T(8,128)(2,1)}), bf16[384,768]{1,0:T(8,128)(2,1)}) %reduce-scatter.69.cloned.1.call-update) | async-done | bytes 589840 | tf_op jit(solution)/shard_map/reduce_scatter | solution.py:340
  824.6 9.0 reduce-scatter.67.cloned.1.call-done
  835.3 107.1 %all-reduce.7.cloned.1.call-done = (bf16[1,384,192]{1,2,0:T(8,128)(2,1)}, bf16[1,384,192]{1,2,0:T(8,128)(2,1)}, bf16[1,384,192]{1,2,0:T(8,128)(2,1)}, bf16[1,384...) async-done(((bf16[1,384,192]{1,2,0:T(8,128)(2,1)}, ...) | async-done | bytes 3538960 | tf_op jit(solution)/shard_map/psum | solution.py:348
  (525 shorter events, 274.6 us)
Async XLA Ops:
  8.0 26.5 %copy-start.57 = (bf16[2,384,192]{1,2,0:T(8,128)(2,1)S(1)}, bf16[2,384,192]{1,2,0:T(8,128)(2,1)}, u32[]{:S(2)}) copy-start(bf16[2,384,192]{1,2,0:T(8,128)(2,1)} %param.25) | copy-start | bytes 884740
  8.0 124.2 %reduce-scatter.45.cloned.1.call-start = ((), (), s32[]{:S(2)}) async-start(), calls=%async_computation.24 | async-start | bytes 983040 | tf_op jit(solution)/shard_map/reduce_scatter | solution.py:28
  8.1 33.6 %copy-start.58 = (bf16[2,192,384]{2,1,0:T(8,128)(2,1)S(1)}, bf16[2,192,384]{2,1,0:T(8,128)(2,1)}, u32[]{:S(2)}) copy-start(bf16[2,192,384]{2,1,0:T(8,128)(2,1)} %param.26) | copy-start | bytes 884740
  26.2 70.2 %copy-start.33 = (bf16[1,768,192]{1,2,0:T(8,128)(2,1)}, bf16[1,768,192]{1,2,0:T(8,128)(2,1)S(1)}, u32[]{:S(2)}) copy-start(bf16[1,768,192]{1,2,0:T(8,128)(2,1)S(1)} %all-gather.2) | copy-start | bytes 884740
  41.7 36.2 %copy-start.28 = (bf16[1,768,192]{1,2,0:T(8,128)(2,1)}, bf16[1,768,192]{1,2,0:T(8,128)(2,1)S(1)}, u32[]{:S(2)}) copy-start(bf16[1,768,192]{1,2,0:T(8,128)(2,1)S(1)} %all-gather) | copy-start | bytes 884740
  47.5 59.5 %copy-start.14 = (bf16[1,192,768]{2,1,0:T(8,128)(2,1)}, bf16[1,192,768]{2,1,0:T(8,128)(2,1)S(1)}, u32[]{:S(2)}) copy-start(bf16[1,192,768]{2,1,0:T(8,128)(2,1)S(1)} %all-gather.5) | copy-start | bytes 884740
  57.7 38.7 %copy-start = (bf16[2,256,768]{2,1,0:T(8,128)(2,1)}, bf16[2,256,768]{2,1,0:T(8,128)(2,1)S(1)}, u32[]{:S(2)}) copy-start(bf16[2,256,768]{2,1,0:T(8,128)(2,1)S(1)} %all_gather.162) | copy-start | bytes 2359300
  109.0 34.1 %all-gather.35.cloned.1.call-start = ((), (), s32[]{:S(2)}) async-start(), calls=%async_computation.38 | async-start | bytes 1769472 | tf_op jit(solution)/shard_map/all_gather | solution.py:56
  110.2 47.2 %all-gather.37.cloned.1.call-start = ((), (), s32[]{:S(2)}) async-start(), calls=%async_computation.39 | async-start | bytes 1769472 | tf_op jit(solution)/shard_map/all_gather | solution.py:57
  111.8 96.1 %reduce-scatter.47.cloned.1.call-start = ((), (), s32[]{:S(2)}) async-start(), calls=%async_computation.25 | async-start | bytes 983040 | tf_op jit(solution)/shard_map/reduce_scatter | solution.py:28
  134.5 73.4 %copy-start.72 = (f32[2,64]{1,0:T(2,128)}, f32[2,64]{1,0:T(2,128)S(1)}, u32[]{:S(2)}) copy-start(f32[2,64]{1,0:T(2,128)S(1)} %fusion.108) | copy-start | bytes 1540
  160.4 47.6 %copy-start.8 = (bf16[2,64,768]{2,1,0:T(8,128)(2,1)S(1)}, bf16[2,64,768]{2,1,0:T(8,128)(2,1)}, u32[]{:S(2)}) copy-start(bf16[2,64,768]{2,1,0:T(8,128)(2,1)} %reduce-scatter.45.cloned.1.call-done) | copy-start | bytes 589828
  160.4 128.0 %reduce-scatter.49.cloned.1.call-start = ((), (), s32[]{:S(2)}) async-start(), calls=%async_computation.26 | async-start | bytes 983040 | tf_op jit(solution)/shard_map/reduce_scatter | solution.py:28
  189.8 66.9 %copy-start.35 = (bf16[1,768,192]{1,2,0:T(8,128)(2,1)}, bf16[1,768,192]{1,2,0:T(8,128)(2,1)S(1)}, u32[]{:S(2)}) copy-start(bf16[1,768,192]{1,2,0:T(8,128)(2,1)S(1)} %all-gather.17) | copy-start | bytes 884740
  201.9 36.3 %copy-start.30 = (bf16[1,768,192]{1,2,0:T(8,128)(2,1)}, bf16[1,768,192]{1,2,0:T(8,128)(2,1)S(1)}, u32[]{:S(2)}) copy-start(bf16[1,768,192]{1,2,0:T(8,128)(2,1)S(1)} %all-gather.15) | copy-start | bytes 884740
  209.1 79.3 %copy-start.70 = (f32[2,64]{1,0:T(2,128)}, f32[2,64]{1,0:T(2,128)S(1)}, u32[]{:S(2)}) copy-start(f32[2,64]{1,0:T(2,128)S(1)} %broadcast_multiply_fusion.2) | copy-start | bytes 1540
  209.4 79.1 %copy-start.74 = (f32[2,64]{1,0:T(2,128)}, f32[2,64]{1,0:T(2,128)S(1)}, u32[]{:S(2)}) copy-start(f32[2,64]{1,0:T(2,128)S(1)} %fusion.109) | copy-start | bytes 1540
  218.1 38.7 %copy-start.3 = (bf16[2,256,768]{2,1,0:T(8,128)(2,1)}, bf16[2,256,768]{2,1,0:T(8,128)(2,1)S(1)}, u32[]{:S(2)}) copy-start(bf16[2,256,768]{2,1,0:T(8,128)(2,1)S(1)} %all_gather.181) | copy-start | bytes 2359300
  262.3 133.1 %copy-start.91 = (f32[2,3,256]{2,1,0:T(4,128)}, f32[2,3,256]{2,1,0:T(4,128)S(1)}, u32[]{:S(2)}) copy-start(f32[2,3,256]{2,1,0:T(4,128)S(1)} %get-tuple-element.123) | copy-start | bytes 18436
  267.6 30.8 %all-gather.39.cloned.1.call-start = ((), (), s32[]{:S(2)}) async-start(), calls=%async_computation.40 | async-start | bytes 1769472 | tf_op jit(solution)/shard_map/all_gather | solution.py:56
  268.2 47.0 %all-gather.41.cloned.1.call-start = ((), (), s32[]{:S(2)}) async-start(), calls=%async_computation.41 | async-start | bytes 1769472 | tf_op jit(solution)/shard_map/all_gather | solution.py:57
  268.9 72.9 %reduce-scatter.51.cloned.1.call-start = ((), (), s32[]{:S(2)}) async-start(), calls=%async_computation.27 | async-start | bytes 983040 | tf_op jit(solution)/shard_map/reduce_scatter | solution.py:28
  318.5 63.7 %reduce-scatter.53.cloned.1.call-start = ((), (), s32[]{:S(2)}) async-start(), calls=%async_computation.28 | async-start | bytes 983040 | tf_op jit(solution)/shard_map/reduce_scatter | solution.py:28
  358.3 69.1 %reduce-scatter.55.cloned.1.call-start = ((), (), s32[]{:S(2)}) async-start(), calls=%async_computation.29 | async-start | bytes 983040 | tf_op jit(solution)/shard_map/reduce_scatter | solution.py:260
  403.5 48.9 %reduce-scatter.57.cloned.1.call-start = ((), (), s32[]{:S(2)}) async-start(), calls=%async_computation.30 | async-start | bytes 983040 | tf_op jit(solution)/shard_map/reduce_scatter | solution.py:263
  408.1 69.5 %reduce-scatter.59.cloned.1.call-start = ((), (), s32[]{:S(2)}) async-start(), calls=%async_computation.31 | async-start | bytes 983040 | tf_op jit(solution)/shard_map/reduce_scatter | solution.py:28
  454.8 35.0 %copy-start.109 = (bf16[1,768,768]{2,1,0:T(8,128)(2,1)S(1)}, bf16[1,768,768]{2,1,0:T(8,128)(2,1)}, u32[]{:S(2)}) copy-start(bf16[1,768,768]{2,1,0:T(8,128)(2,1)} %all-gather.37.cloned.1.call-done) | copy-start | bytes 3538948
  454.8 63.3 %reduce-scatter.61.cloned.1.call-start = ((), (), s32[]{:S(2)}) async-start(), calls=%async_computation.32 | async-start | bytes 983040 | tf_op jit(solution)/shard_map/reduce_scatter | solution.py:28
  492.4 25.6 %copy-start.9 = (bf16[2,64,768]{2,1,0:T(8,128)(2,1)S(1)}, bf16[2,64,768]{2,1,0:T(8,128)(2,1)}, u32[]{:S(2)}) copy-start(bf16[2,64,768]{2,1,0:T(8,128)(2,1)} %reduce-scatter.45.cloned.1.call-done) | copy-start | bytes 589828
  492.4 25.6 %copy-start.73 = (f32[2,64]{1,0:T(2,128)S(1)}, f32[2,64]{1,0:T(2,128)}, u32[]{:S(2)}) copy-start(f32[2,64]{1,0:T(2,128)} %copy-done.72) | copy-start | bytes 1540
  494.1 25.8 %copy-start.85 = (f32[2,64]{1,0:T(2,128)S(1)}, f32[2,64]{1,0:T(2,128)}, u32[]{:S(2)}) copy-start(f32[2,64]{1,0:T(2,128)} %copy-done.84) | copy-start | bytes 1540
  494.2 85.6 %reduce-scatter.65.cloned.1.call-start = ((), (), s32[]{:S(2)}) async-start(), calls=%async_computation.34 | async-start | bytes 983040 | tf_op jit(solution)/shard_map/reduce_scatter | solution.py:263
  535.9 49.3 %reduce-scatter.63.cloned.1.call-start = ((), (), s32[]{:S(2)}) async-start(), calls=%async_computation.33 | async-start | bytes 983040 | tf_op jit(solution)/shard_map/reduce_scatter | solution.py:260
  544.8 55.7 %reduce-scatter.87.cloned.1.call-start = ((), (), s32[]{:S(2)}) async-start(), calls=%async_computation.49 | async-start | bytes 589824
  549.1 67.5 %reduce-scatter.75.cloned.1.call-start = ((), (), s32[]{:S(2)}) async-start(), calls=%async_computation.43 | async-start | bytes 589824
  553.3 87.2 %reduce-scatter.91.cloned.1.call-start = ((), (), s32[]{:S(2)}) async-start(), calls=%async_computation.51 | async-start | bytes 1769472
  559.0 96.9 %reduce-scatter.83.cloned.1.call-start = ((), (), s32[]{:S(2)}) async-start(), calls=%async_computation.47 | async-start | bytes 589824
  563.3 108.5 %reduce-scatter.79.cloned.1.call-start = ((), (), s32[]{:S(2)}) async-start(), calls=%async_computation.45 | async-start | bytes 589824
  567.5 119.7 %reduce-scatter.85.cloned.1.call-start = ((), (), s32[]{:S(2)}) async-start(), calls=%async_computation.48 | async-start | bytes 589824
  571.8 131.4 %reduce-scatter.73.cloned.1.call-start = ((), (), s32[]{:S(2)}) async-start(), calls=%async_computation.42 | async-start | bytes 589824
  576.2 151.1 %reduce-scatter.89.cloned.1.call-start = ((), (), s32[]{:S(2)}) async-start(), calls=%async_computation.50 | async-start | bytes 1769472
  579.7 163.1 %reduce-scatter.81.cloned.1.call-start = ((), (), s32[]{:S(2)}) async-start(), calls=%async_computation.46 | async-start | bytes 589824
  582.0 176.8 %reduce-scatter.77.cloned.1.call-start = ((), (), s32[]{:S(2)}) async-start(), calls=%async_computation.44 | async-start | bytes 589824
  587.4 195.8 %reduce-scatter.71.cloned.1.call-start = ((), (), s32[]{:S(2)}) async-start(), calls=%async_computation.37 | async-start | bytes 1769472 | tf_op jit(solution)/shard_map/reduce_scatter | solution.py:340
  589.4 218.4 %reduce-scatter.69.cloned.1.call-start = ((), (), s32[]{:S(2)}) async-start(), calls=%async_computation.36 | async-start | bytes 1769472 | tf_op jit(solution)/shard_map/reduce_scatter | solution.py:340
  592.6 215.3 %all-reduce.5.cloned.1.call-start = ((), (), s32[]{:S(2)}) async-start(), calls=%async_computation.52 | async-start | bytes 180224 | tf_op jit(solution)/shard_map/psum | solution.py:355
  595.6 237.9 %reduce-scatter.67.cloned.1.call-start = ((), (), s32[]{:S(2)}) async-start(), calls=%async_computation.35 | async-start | bytes 983040 | tf_op jit(solution)/shard_map/reduce_scatter | solution.py:28
  597.7 344.7 %all-reduce.7.cloned.1.call-start = ((), (), s32[]{:S(2)}) async-start(), calls=%async_computation.53 | async-start | bytes 7077888 | tf_op jit(solution)/shard_map/psum | solution.py:348
  (99 other events, 752.3 us)
Sparse Core Ops, SparseCore 0:
  109.1 21.5 reduce-scatter.44
  160.5 23.2 reduce-scatter.46
  267.7 20.6 reduce-scatter.48
  318.6 23.2 reduce-scatter.50
  358.4 23.7 reduce-scatter.52
  454.9 22.6 reduce-scatter.58
  494.3 23.7 reduce-scatter.60
  600.4 150.4 all-reduce.4
  808.0 134.3 all-reduce.6
Sparse Core Ops, SparseCore 1:
  111.6 21.1 all-gather.34
  134.7 22.6 all-gather.36
  270.2 20.2 all-gather.38
  292.6 22.5 all-gather.40
  403.6 23.8 reduce-scatter.54
  429.7 22.6 reduce-scatter.56
  536.0 23.7 reduce-scatter.64
  562.6 22.6 reduce-scatter.62
  587.9 12.5 reduce-scatter.86
  603.3 13.1 reduce-scatter.74
  618.7 21.8 reduce-scatter.90
  642.8 13.1 reduce-scatter.82
  658.6 13.1 reduce-scatter.78
  674.0 13.1 reduce-scatter.84
  690.0 13.1 reduce-scatter.72
  705.5 21.8 reduce-scatter.88
  729.6 13.1 reduce-scatter.80
  745.6 13.1 reduce-scatter.76
  761.4 21.7 reduce-scatter.70
  786.1 21.7 reduce-scatter.68
  810.3 23.2 reduce-scatter.66
where the time goes:
time: 969 us; the launch traced here: 958 us
  waiting for transfers between devices  449 us (46%)
  blocking collectives  271 us (28%)
  matrix products  99.4 us (10%)
  local copies, waits for them, and re-layouts  68.3 us (7%)
  other arithmetic  50.8 us (5%)
  between operations  17.4 us (2%)
    unnamed x40, waiting for transfers between devices  146 us
    psum x1, waiting for transfers between devices, reduce_grads(): lax.psum(part_query.astype(jnp.bfloat16), 'ctx').astype(jnp.float32)  107 us
    reduce_scatter x8, waiting for transfers between devices, rows_sum(): lax.psum_scatter(partial_rows.astype(jnp.bfloat16), 'tp', scatter_dimensi...  91.1 us
    all_gather x8, blocking collectives, rows_all(): return lax.all_gather(local_rows, 'tp', axis=1, tiled=True)  65.6 us
    reduce_scatter x2, waiting for transfers between devices, reduce_grads(): lax.psum_scatter(mat_inner.astype(jnp.bfloat16), 'shard', scatter_dimensi...  47.4 us
    unnamed x254, local copies, waits for them, and re-layouts  43 us
    all_gather x2, blocking collectives, layer_forward(): lax.all_gather(key_rows, 'ctx', axis=1, tiled=True)  39.5 us
    all_gather x2, blocking collectives, layer_forward(): lax.all_gather(value_rows, 'ctx', axis=1, tiled=True)  36.2 us
  transfers between devices with their start and end apart: 30, of which 24 were waited for; matrix products, arithmetic and copies ran while one was open for 13% of the time, Pallas kernels for 0%

commit v1 on v0

v1 whole, which is shorter than its diff:
```python
import functools

import jax
import jax.numpy as jnp
from jax import lax
from jax.experimental import pallas as pl
from jax.experimental.pallas import tpu as pltpu
from jax.sharding import PartitionSpec as P

HD = 64
LAYERS = 2
EPSILON = 1e-05
MESH = pl.DeviceIdType.MESH
F32 = jnp.float32
BF16 = jnp.bfloat16
NEG = -1e30
VEC_ROWS = 24


def nn(a, b):
    return jnp.dot(a, b, preferred_element_type=F32)


def nt(a, b):
    return lax.dot_general(a, b, (((1,), (1,)), ((), ())), preferred_element_type=F32)


def tn(a, b):
    return lax.dot_general(a, b, (((0,), (0,)), ((), ())), preferred_element_type=F32)


def norm_forward(resid, gain, shift):
    center = resid - jnp.mean(resid, axis=-1, keepdims=True)
    spread = jnp.mean(center * center, axis=-1, keepdims=True)
    rstd = lax.rsqrt(spread + EPSILON)
    xhat = center * rstd
    return xhat * gain + shift, xhat, rstd


def norm_backward(grad, xhat, rstd, gain):
    scaled = grad * gain
    first = jnp.mean(scaled, axis=-1, keepdims=True)
    second = jnp.mean(scaled * xhat, axis=-1, keepdims=True)
    return rstd * (scaled - first - xhat * second)


def step_kernel(dims, fused, *refs):
    (
        tok_ref,
        cot_ref,
        idc_ref,
        idr_ref,
        vec_ref,
        wq_ref,
        wk_ref,
        wv_ref,
        wo_ref,
        wi_ref,
        wu_ref,
        out_tok,
        out_grad,
        out_mat,
        out_vec,
        WQ,
        WK,
        WV,
        WO,
        WI,
        WU,
        VB,
        H,
        N1,
        DR,
        DR1,
        TK,
        CO,
        OT,
        OG,
        XH1,
        XH2,
        SD1,
        SD2,
        XB,
        Q,
        K,
        V,
        OB,
        N1B,
        G,
        GP,
        PB,
        DF,
        DA,
        DU,
        DOB,
        DQ,
        DK,
        DV,
        DKF,
        DVF,
        PF,
        SB,
        RB,
        ZS,
        ZR,
        GO,
        GS,
        XR,
        YR,
        Y2,
        wl_sem,
        ws_sem,
        wr_sem,
        rd_s,
        rd_r,
        g8_s,
        g8_r,
        g4_s,
        g4_r,
        rs_s,
        rs_r,
        rz_s,
        rz_r,
        xs_s,
        xs_r,
        z1_s,
        z1_r,
        z2_s,
        z2_r,
        z3_s,
        z3_r,
        om_sem,
    ) = refs
    width, cols, units, half = dims
    seqs, part = tok_ref.shape[0], tok_ref.shape[1]
    rows = 2 * part
    own_rows = 4 * rows
    all_rows = 8 * rows
    s = lax.axis_index("shard")
    c = lax.axis_index("ctx")
    t = lax.axis_index("tp")
    hf = lax.rem(c, 2)
    y = t // 2
    k = lax.rem(t, 2)
    tc = t + 1 - 2 * k
    ty = lax.rem(t + 2, 4)
    zp = c + 1 - 2 * hf
    is_inner = jnp.logical_or(c == 1, c == 2)
    is_outer = jnp.logical_not(is_inner)
    z_in = jnp.where(c == 0, 1, 2)
    z_mid = 3 - c
    z_out = jnp.where(c == 1, 0, 3)

    def rc(src, dst, ssem, rsem, cc, tt, ss=None):
        return pltpu.make_async_remote_copy(
            src_ref=src,
            dst_ref=dst,
            send_sem=ssem,
            recv_sem=rsem,
            device_id=(s if ss is None else ss, cc, tt),
            device_id_type=MESH,
        )

    bar = pltpu.get_barrier_semaphore()
    for dc in range(4):
        for dt in range(4):
            if dc or dt:
                pl.semaphore_signal(
                    bar,
                    1,
                    device_id=(s, lax.rem(c + dc, 4), lax.rem(t + dt, 4)),
                    device_id_type=MESH,
                )
    if fused:
        pl.semaphore_signal(bar, 1, device_id=(1 - s, c, t), device_id_type=MESH)
    pl.semaphore_wait(bar, 16 if fused else 15)

    row_at = pl.multiple_of(s * half, half)

    def weight_views(layer):
        if not fused:
            return [
                (wq_ref.at[layer], WQ.at[layer]),
                (wk_ref.at[layer], WK.at[layer]),
                (wv_ref.at[layer], WV.at[layer]),
                (wo_ref.at[layer], WO.at[layer]),
                (wi_ref.at[layer], WI.at[layer]),
                (wu_ref.at[layer], WU.at[layer]),
            ]
        return [
            (wq_ref.at[layer], WQ.at[layer, pl.ds(row_at, half)]),
            (wk_ref.at[layer], WK.at[layer, pl.ds(row_at, half)]),
            (wv_ref.at[layer], WV.at[layer, pl.ds(row_at, half)]),
            (wo_ref.at[layer], WO.at[layer, :, pl.ds(row_at, half)]),
            (wi_ref.at[layer], WI.at[layer, pl.ds(row_at, half)]),
            (wu_ref.at[layer], WU.at[layer, :, pl.ds(row_at, half)]),
        ]

    def weight_copies(layer, item):
        src, dst = weight_views(layer)[item]
        local = pltpu.make_async_copy(src, dst, wl_sem.at[layer, item])
        remote = None
        if fused:
            remote = rc(src, dst, ws_sem.at[layer, item], wr_sem.at[layer, item], c, t, 1 - s)
        return local, remote

    def weight_wait(layer, item):
        local, remote = weight_copies(layer, item)
        local.wait()
        if fused:
            remote.wait()

    if fused:
        vec_copy = rc(vec_ref, VB.at[s], ws_sem.at[0, 6], wr_sem.at[0, 6], c, t, 1 - s)
        vec_copy.start()
        VB[s] = vec_ref[...]
    else:
        VB[...] = vec_ref[...]

    b_me = c // 2
    spread_t = 2 * hf + y

    def spread_copies(src_ref, dst_ref, which):
        return [
            (
                jnp.logical_and(2 * b + c // 2 == c, spread_t == t),
                rc(
                    src_ref.at[b],
                    dst_ref.at[pl.ds(k * part, part)],
                    rd_s.at[which, b],
                    rd_r.at[which, k],
                    2 * b + c // 2,
                    spread_t,
                ),
            )
            for b in range(2)
        ]

    def spread_start(src_ref, dst_ref, which):
        for b, (mine, copy) in enumerate(spread_copies(src_ref, dst_ref, which)):

            @pl.when(mine)
            def _():
                dst_ref[pl.ds(pl.multiple_of(k * part, part), part), :] = src_ref[b]

            @pl.when(jnp.logical_not(mine))
            def _():
                copy.start()

    def spread_wait(src_ref, dst_ref, which):
        for mine, copy in spread_copies(src_ref, dst_ref, which):

            @pl.when(jnp.logical_not(mine))
            def _():
                copy.wait_send()

        for kk in range(2):
            mine = jnp.logical_and(2 * hf + y == c, 2 * k + kk == t)

            @pl.when(jnp.logical_not(mine))
            def _():
                rc(
                    src_ref.at[0],
                    dst_ref.at[pl.ds(kk * part, part)],
                    rd_s.at[which, 0],
                    rd_r.at[which, kk],
                    c,
                    t,
                ).wait_recv()

    def collect_copies(src_ref, dst_ref, which):
        return [
            (
                jnp.logical_and(2 * hf + y == c, 2 * k + kk == t),
                rc(
                    src_ref.at[pl.ds(kk * part, part)],
                    dst_ref.at[b_me],
                    rd_s.at[which, kk],
                    rd_r.at[which, b_me],
                    2 * hf + y,
                    2 * k + kk,
                ),
            )
            for kk in range(2)
        ]

    def collect_start(src_ref, dst_ref, which):
        for kk, (mine, copy) in enumerate(collect_copies(src_ref, dst_ref, which)):

            @pl.when(mine)
            def _():
                dst_ref[b_me] = src_ref[kk * part : (kk + 1) * part, :]

            @pl.when(jnp.logical_not(mine))
            def _():
                copy.start()

    def collect_wait(src_ref, dst_ref, which):
        for mine, copy in collect_copies(src_ref, dst_ref, which):

            @pl.when(jnp.logical_not(mine))
            def _():
                copy.wait_send()

        for b in range(2):
            mine = jnp.logical_and(2 * b + c // 2 == c, spread_t == t)

            @pl.when(jnp.logical_not(mine))
            def _():
                rc(
                    src_ref.at[pl.ds(0, part)],
                    dst_ref.at[b],
                    rd_s.at[which, 0],
                    rd_r.at[which, b],
                    c,
                    t,
                ).wait_recv()

    spread_start(tok_ref, TK, 0)
    for layer in range(LAYERS):
        for item in range(6):
            local, remote = weight_copies(layer, item)
            local.start()
            if fused:
                remote.start()
    spread_start(cot_ref, CO, 1)

    def gather_copies(buf, ssem, rsem):
        return (
            rc(buf.at[t], buf.at[t], ssem.at[0], rsem.at[0], c, tc),
            rc(buf.at[t], buf.at[t], ssem.at[1], rsem.at[1], c, ty),
            rc(buf.at[ty], buf.at[ty], ssem.at[2], rsem.at[2], c, tc),
        )

    def gather_start(copies):
        copies[1].start()
        copies[0].start()

    def gather_remote(copies):
        copies[1].wait_recv()
        copies[2].start()
        copies[2].wait_recv()

    def gather_finish(copies):
        for copy in copies:
            copy.wait_send()

    def sum_copies(slot, lane):
        return (
            rc(SB.at[lane, 0], RB.at[slot, 0], rs_s.at[slot, 0], rs_r.at[slot, 0], c, tc),
            rc(SB.at[lane, 1], RB.at[slot, 1], rs_s.at[slot, 1], rs_r.at[slot, 1], c, ty),
            rc(SB.at[lane, 2], RB.at[slot, 2], rs_s.at[slot, 2], rs_r.at[slot, 2], c, tc),
        )

    def sum_remote(copies, pf, slot, lane):
        SB[lane, 0] = pf[(1 - y) * 2 + 1 - k].astype(BF16)
        copies[0].start()
        copies[0].wait_recv()
        SB[lane, 1] = (pf[ty] + RB[slot, 0].astype(F32)).astype(BF16)
        copies[1].start()

    def sum_local(copies, pf, slot, lane):
        SB[lane, 2] = pf[tc].astype(BF16)
        copies[2].start()

    def sum_finish(copies, pf, slot, lane):
        copies[2].wait_recv()
        partial = pf[t] + RB[slot, 2].astype(F32)
        copies[1].wait_recv()
        for copy in copies:
            copy.wait_send()
        return partial + RB[slot, 1].astype(F32)

    def full_vec(layer, row):
        return jnp.concatenate([VB[0, layer, row : row + 1], VB[1, layer, row : row + 1]], axis=1)

    def vec_at(layer, row, lanes):
        return VB[y, layer, pl.ds(row, 1)][:, :lanes]

    out_vec[...] = jnp.zeros_like(out_vec)

    def put_vec(layer, row, value):
        out_vec[layer, pl.ds(row, 1), : value.shape[1]] = value

    if fused:
        vec_copy.wait()
    spread_wait(tok_ref, TK, 0)
    H[...] = TK[...].astype(F32)
    lane_low = lax.broadcasted_iota(jnp.int32, (1, 2 * HD), 1) < HD

    def head_cols(value, head):
        if head == 2:
            return value[:, 2 * HD : 3 * HD]
        keep = lane_low if head == 0 else jnp.logical_not(lane_low)
        return jnp.where(keep, value[:, : 2 * HD], jnp.zeros_like(value[:, : 2 * HD]))

    def head_full(value, head):
        return value[:, 2 * HD : 3 * HD] if head == 2 else value[:, : 2 * HD]

    tile = own_rows // 2

    def forward_layer(layer, carry):
        buf = XB.at[layer]
        own = hf * 4
        far = (1 - hf) * 4
        ss, rr = g8_s.at[layer], g8_r.at[layer]
        XB[layer, own + t] = H[...].astype(BF16)
        to_y = rc(buf.at[own + t], buf.at[own + t], ss.at[0], rr.at[0], c, ty)
        to_z = rc(buf.at[own + t], buf.at[own + t], ss.at[1], rr.at[1], zp, t)
        to_c = rc(buf.at[own + t], buf.at[own + t], ss.at[2], rr.at[2], c, tc)
        y_to_c = rc(buf.at[own + ty], buf.at[own + ty], ss.at[3], rr.at[3], c, tc)
        z_to_y = rc(buf.at[far + t], buf.at[far + t], ss.at[4], rr.at[4], c, ty)
        z_to_c = rc(buf.at[far + t], buf.at[far + t], ss.at[5], rr.at[5], c, tc)
        zy_to_c = rc(buf.at[far + ty], buf.at[far + ty], ss.at[6], rr.at[6], c, tc)
        to_y.start()
        to_z.start()
        to_c.start()
        for item in range(3):
            weight_wait(layer, item)

        def project(at, with_q):
            block = XB[layer, pl.ds(at, 2)].reshape(2 * rows, width)
            where = pl.ds(pl.multiple_of(at * rows, 2 * rows), 2 * rows)
            if with_q:
                mine = pl.ds(pl.multiple_of((at - own) * rows, 2 * rows), 2 * rows)
                qb = vec_at(layer, k, cols)
                q_low = (nn(block, WQ[layer]) + qb).astype(BF16)
                Q[layer, mine] = q_low * jnp.asarray(HD**-0.5, BF16)
            K[layer, where] = nn(block, WK[layer]).astype(BF16)
            V[layer, where] = (nn(block, WV[layer]) + vec_at(layer, 2 + k, cols)).astype(BF16)

        to_c.wait_recv()
        project(own + 2 * y, True)
        to_z.wait_recv()
        z_to_y.start()
        z_to_c.start()
        to_y.wait_recv()
        y_to_c.start()
        y_to_c.wait_recv()
        project(own + 2 * (1 - y), True)
        z_to_c.wait_recv()
        project(far + 2 * y, False)
        z_to_y.wait_recv()
        zy_to_c.start()
        zy_to_c.wait_recv()
        project(far + 2 * (1 - y), False)
        for copy in (to_y, to_z, to_c, y_to_c, z_to_y, z_to_c, zy_to_c):
            copy.wait_send()

        def attend(at, inner):
            where = pl.ds(pl.multiple_of(at * tile, tile), tile)
            ids = idc_ref[where][:, :1] == idr_ref[:1]
            q_tile = Q[layer, where]
            mixed = []
            for head in range(3):
                scores = nt(head_cols(q_tile, head), head_full(K[layer], head))
                scores = jnp.where(ids, scores, NEG)
                top = jnp.max(scores, axis=-1, keepdims=True)
                expo = jnp.exp(scores - top)
                low = (expo / jnp.sum(expo, axis=-1, keepdims=True)).astype(BF16)
                PB[layer, head, where] = low
                mixed.append(nn(low, head_full(V[layer], head)))
            OB[layer, where, : 2 * HD] = jnp.where(lane_low, mixed[0], mixed[1]).astype(BF16)
            OB[layer, where, 2 * HD :] = mixed[2].astype(BF16)
            return inner

        lax.fori_loop(0, 2, attend, 0)
        weight_wait(layer, 3)

        def project_out(at):
            where = pl.ds(pl.multiple_of(at * 2 * rows, 2 * rows), 2 * rows)
            PF[pl.ds(at * 2, 2)] = nn(OB[layer, where], WO[layer]).reshape(2, rows, width)

        copies = sum_copies(0, 0)
        project_out(1 - y)
        sum_remote(copies, PF, 0, 0)
        project_out(y)
        sum_local(copies, PF, 0, 0)
        branch = sum_finish(copies, PF, 0, 0) + full_vec(layer, 4)
        normed, xhat, rstd = norm_forward(H[...] + branch, full_vec(layer, 6), full_vec(layer, 7))
        N1[...] = normed
        XH1[layer] = xhat
        SD1[layer] = jnp.broadcast_to(rstd, (rows, 128))

        N1B[layer, t] = normed.astype(BF16)
        moves = gather_copies(N1B.at[layer], g4_s.at[layer, 0], g4_r.at[layer, 0])
        gather_start(moves)
        weight_wait(layer, 4)
        weight_wait(layer, 5)

        def feed(at):
            where = pl.ds(pl.multiple_of(at * 2 * rows, 2 * rows), 2 * rows)
            block = N1B[layer, pl.ds(at * 2, 2)].reshape(2 * rows, width)
            bias = jnp.concatenate([vec_at(layer, 10 + 2 * k, half), vec_at(layer, 11 + 2 * k, half)], axis=1)
            pre = nn(block, WI[layer]) + bias
            phi = 0.5 * (1.0 + lax.erf(pre * (0.5**0.5)))
            low = (pre * phi).astype(BF16)
            G[layer, where] = low
            density = jnp.exp(pre * pre * -0.5) * ((0.5 / jnp.pi) ** 0.5)
            GP[layer, where] = (phi + pre * density).astype(GP.dtype)
            PF[pl.ds(at * 2, 2)] = nn(low, WU[layer]).reshape(2, rows, width)

        copies = sum_copies(1, 0)
        moves[0].wait_recv()
        feed(y)
        sum_local(copies, PF, 1, 0)
        gather_remote(moves)
        feed(1 - y)
        sum_remote(copies, PF, 1, 0)
        gather_finish(moves)
        second = N1[...] + sum_finish(copies, PF, 1, 0) + full_vec(layer, 5)
        result, xhat, rstd = norm_forward(second, full_vec(layer, 8), full_vec(layer, 9))
        XH2[layer] = xhat
        SD2[layer] = jnp.broadcast_to(rstd, (rows, 128))
        H[...] = result
        return carry

    for layer in range(LAYERS):
        forward_layer(layer, 0)

    TK[...] = H[...].astype(BF16)
    collect_start(TK, OT, 2)
    spread_wait(cot_ref, CO, 1)
    H[...] = CO[...].astype(F32)

    first_half = row_at if fused else 0
    other_half = pl.multiple_of((1 - s) * half, half) if fused else half

    def split_grad(a, b_ref_at, unit, step, count):
        for own_side in (True, False):
            at = first_half if own_side else other_half
            value = tn(a, b_ref_at(at)).astype(BF16)
            value = value.reshape(count, cols, half)
            if own_side:
                GO[pl.ds(unit, count)] = value
            elif fused:
                GS[pl.ds(step, count)] = value
            else:
                XR[pl.ds(unit, count)] = value

    def backward_layer(layer):
        base = (LAYERS - 1 - layer) * 12
        grad = H[...]
        xhat = XH2[layer]
        rstd = SD2[layer][:, :1]
        d_second = norm_backward(grad, xhat, rstd, full_vec(layer, 8))
        put_vec(layer, 4, jnp.sum(grad * xhat, axis=0, keepdims=True))
        put_vec(layer, 5, jnp.sum(grad, axis=0, keepdims=True))
        DR[...] = d_second
        DF[t] = d_second.astype(BF16)
        moves = gather_copies(DF, g4_s.at[layer, 1], g4_r.at[layer, 1])
        gather_start(moves)
        copies = sum_copies(2, 0)

        def back_feed(at):
            where = pl.ds(pl.multiple_of(at * 2 * rows, 2 * rows), 2 * rows)
            block = DF[pl.ds(at * 2, 2)].reshape(2 * rows, width)
            d_act = nt(block, WU[layer])
            low = (d_act * GP[layer, where].astype(F32)).astype(BF16)
            DU[where] = low
            PF[pl.ds(at * 2, 2)] = nt(low, WI[layer]).reshape(2, rows, width)

        moves[0].wait_recv()
        back_feed(y)
        sum_local(copies, PF, 2, 0)
        gather_remote(moves)
        back_feed(1 - y)
        sum_remote(copies, PF, 2, 0)
        gather_finish(moves)

        def halves(ref):
            return lambda at: ref[:, :, pl.ds(at, half)].reshape(-1, half)

        split_grad(G[layer], halves(DF), base, 0, 4)
        split_grad(DU[...], halves(N1B.at[layer]), base + 4, 4, 4)
        only = jnp.where(t == 0, 1.0, 0.0)
        put_vec(layer, 0, only * jnp.sum(DF[...].reshape(own_rows, width).astype(F32), axis=0, keepdims=True))
        put_vec(layer, 14 + t, jnp.sum(DU[...].astype(F32), axis=0, keepdims=True))

        d_normed = DR[...] + sum_finish(copies, PF, 2, 0)
        xhat = XH1[layer]
        d_first = norm_backward(d_normed, xhat, SD1[layer][:, :1], full_vec(layer, 6))
        put_vec(layer, 2, jnp.sum(d_normed * xhat, axis=0, keepdims=True))
        put_vec(layer, 3, jnp.sum(d_normed, axis=0, keepdims=True))
        DR1[...] = d_first
        DA[t] = d_first.astype(BF16)
        moves = gather_copies(DA, g4_s.at[layer, 2], g4_r.at[layer, 2])
        gather_start(moves)

        def back_out(at):
            where = pl.ds(pl.multiple_of(at * 2 * rows, 2 * rows), 2 * rows)
            block = DA[pl.ds(at * 2, 2)].reshape(2 * rows, width)
            DOB[where] = nt(block, WO[layer]).astype(BF16)

        moves[0].wait_recv()
        back_out(y)
        gather_remote(moves)
        back_out(1 - y)
        gather_finish(moves)
        split_grad(OB[layer], halves(DA), base + 8, 8, 1)
        put_vec(layer, 1, only * jnp.sum(DA[...].reshape(own_rows, width).astype(F32), axis=0, keepdims=True))

        DKF[...] = jnp.zeros_like(DKF)
        DVF[...] = jnp.zeros_like(DVF)

        def back_attend(at, inner):
            where = pl.ds(pl.multiple_of(at * tile, tile), tile)
            grad_tile = DOB[where]
            q_tile = Q[layer, where]
            product = grad_tile.astype(F32) * OB[layer, where].astype(F32)
            d_query = []
            for head in range(3):
                lanes = slice(2 * HD, 3 * HD) if head == 2 else slice(0, 2 * HD)
                d_mix = head_cols(grad_tile, head)
                d_prob = nt(d_mix, head_full(V[layer], head))
                total = jnp.sum(head_cols(product, head), axis=-1, keepdims=True)
                low = PB[layer, head, where]
                d_score = (low.astype(F32) * (d_prob - total)).astype(BF16)
                d_query.append(nn(d_score, head_full(K[layer], head)))
                DKF[:, lanes] += tn(d_score, head_cols(q_tile, head))
                DVF[:, lanes] += tn(low, d_mix)
            scale = HD**-0.5
            DQ[where, : 2 * HD] = (jnp.where(lane_low, d_query[0], d_query[1]) * scale).astype(BF16)
            DQ[where, 2 * HD :] = (d_query[2] * scale).astype(BF16)
            return inner

        lax.fori_loop(0, 2, back_attend, 0)
        DK[...] = DKF[...].astype(BF16)
        DV[...] = DVF[...].astype(BF16)
        own = hf * 4
        far = (1 - hf) * 4

        def back_in(at, with_q):
            where = pl.ds(pl.multiple_of(at * rows, 2 * rows), 2 * rows)
            total = nt(DK[where], WK[layer]) + nt(DV[where], WV[layer])
            if with_q:
                mine = pl.ds(pl.multiple_of((at - own) * rows, 2 * rows), 2 * rows)
                total = total + nt(DQ[mine], WQ[layer])
            PF[pl.ds(at, 2)] = total.reshape(2, rows, width)

        pf_far = PF.at[pl.ds(far, 4)]
        pf_own = PF.at[pl.ds(own, 4)]
        far_copies = sum_copies(3, 1)
        back_in(far + 2 * (1 - y), False)
        sum_remote(far_copies, pf_far, 3, 1)
        back_in(far + 2 * y, False)
        sum_local(far_copies, pf_far, 3, 1)
        copies = sum_copies(4, 0)
        back_in(own + 2 * (1 - y), True)
        sum_remote(copies, pf_own, 4, 0)
        back_in(own + 2 * y, True)
        sum_local(copies, pf_own, 4, 0)
        ZS[...] = sum_finish(far_copies, pf_far, 3, 1).astype(BF16)
        across = rc(ZS, ZR.at[layer], rz_s.at[layer], rz_r.at[layer], zp, t)
        across.start()

        def block_cols(ref, start, count):
            return lambda at: ref[pl.ds(start, count), :, pl.ds(at, half)].reshape(-1, half)

        xb = XB.at[layer]
        split_grad(DQ[...], block_cols(xb, own, 4), base + 9, 9, 1)
        split_grad(DK[...], block_cols(xb, 0, 8), base + 10, 10, 1)
        split_grad(DV[...], block_cols(xb, 0, 8), base + 11, 11, 1)
        put_vec(layer, 6 + t, jnp.sum(DQ[...].astype(F32), axis=0, keepdims=True))
        put_vec(layer, 10 + t, jnp.sum(DV[...].astype(F32), axis=0, keepdims=True))

        near = sum_finish(copies, pf_own, 4, 0)
        across.wait()
        H[...] = DR1[...] + near + ZR[layer].astype(F32)

    def x_copy(unit, step):
        return rc(GS.at[step], XR.at[unit], xs_s.at[unit], xs_r.at[unit], c, t, 1 - s)

    def z1_copy(unit):
        return rc(GO.at[unit], YR.at[unit], z1_s.at[unit], z1_r.at[unit], z_in, t)

    def z2_copy(unit):
        return rc(GO.at[unit], Y2.at[unit], z2_s.at[unit], z2_r.at[unit], z_mid, t)

    def z3_copy(unit):
        return rc(GO.at[unit], YR.at[unit], z3_s.at[unit], z3_r.at[unit], z_out, t)

    def add_into(unit, other):
        GO[unit] = (GO[unit].astype(F32) + other.astype(F32)).astype(BF16)

    def stage_x(unit, step):
        x_copy(unit, step).start()

    def stage_z1(unit, step):
        copy = x_copy(unit, step)
        copy.wait()
        add_into(unit, XR[unit])

        @pl.when(is_outer)
        def _():
            z1_copy(unit).start()

    def stage_z2(unit):
        @pl.when(is_inner)
        def _():
            z1_copy(unit).wait_recv()
            add_into(unit, YR[unit])
            z2_copy(unit).start()

        @pl.when(is_outer)
        def _():
            z1_copy(unit).wait_send()

    def stage_z3(unit):
        @pl.when(is_inner)
        def _():
            z2_copy(unit).wait()
            add_into(unit, Y2[unit])
            z3_copy(unit).start()

    def stage_out(unit):
        @pl.when(is_inner)
        def _():
            z3_copy(unit).wait_send()
            pltpu.make_async_copy(GO.at[unit], out_mat.at[unit], om_sem.at[unit]).start()

        @pl.when(is_outer)
        def _():
            z3_copy(unit).wait_recv()
            pltpu.make_async_copy(YR.at[unit], out_mat.at[unit], om_sem.at[unit]).start()

    for layer in reversed(range(LAYERS)):
        backward_layer(layer)
        if fused:
            base = (LAYERS - 1 - layer) * 12

            def x_all(i, carry):
                stage_x(base + i, i)
                return carry

            def z1_all(i, carry):
                stage_z1(base + i, i)
                return carry

            lax.fori_loop(0, 12, x_all, 0)
            lax.fori_loop(0, 12, z1_all, 0)

    TK2 = CO
    TK2[...] = H[...].astype(BF16)
    collect_start(TK2, OG, 3)
    total_units = 12 * LAYERS
    if fused:
        for stage in (stage_z2, stage_z3, stage_out):

            def run(i, carry, stage=stage):
                stage(i)
                return carry

            lax.fori_loop(0, total_units, run, 0)

        def drain(i, carry):
            pltpu.make_async_copy(GO.at[i], out_mat.at[i], om_sem.at[i]).wait()
            return carry

        lax.fori_loop(0, total_units, drain, 0)
    else:
        own_out = pltpu.make_async_copy(GO, out_mat.at[0], om_sem.at[0])
        far_out = pltpu.make_async_copy(XR, out_mat.at[1], om_sem.at[1])
        own_out.start()
        far_out.start()
        own_out.wait()
        far_out.wait()
    collect_wait(TK, OT, 2)
    out_tok[...] = OT[...]
    collect_wait(TK2, OG, 3)
    out_grad[...] = OG[...]


def pack_vectors(qb, vb, ob, ub, ib, g1, s1, g2, s2, cols, half):
    def narrow(vec):
        two = vec.astype(F32).reshape(LAYERS, -1, cols)
        return jnp.pad(two, ((0, 0), (0, 0), (0, half - cols)))

    def wide(vec):
        return vec.astype(F32).reshape(LAYERS, -1, half)

    packed = jnp.concatenate(
        [narrow(qb), narrow(vb), wide(ob), wide(ub), wide(g1), wide(s1), wide(g2), wide(s2), wide(ib)], axis=1
    )
    return jnp.pad(packed, ((0, 0), (0, 16 - packed.shape[1]), (0, 0)))


def per_device(
    tokens,
    cotangent,
    segment_ids,
    lengths,
    query_weight,
    key_weight,
    value_weight,
    output_weight,
    inner_weight,
    outer_weight,
    query_bias,
    value_bias,
    output_bias,
    inner_bias,
    outer_bias,
    first_gain,
    first_shift,
    second_gain,
    second_shift,
):
    shards = lax.axis_size("shard")
    assert lax.axis_size("ctx") == 4 and lax.axis_size("tp") == 4 and tokens.shape[0] == 2
    fused = shards == 2
    seqs, part, width = tokens.shape
    cols = query_weight.shape[2]
    units = inner_weight.shape[2]
    half = width // 2
    rows = 2 * part
    own_rows, all_rows = 4 * rows, 8 * rows
    assert cols == 3 * HD and segment_ids.shape[1] == all_rows and units == width == 4 * cols

    c = lax.axis_index("ctx")
    positions = lax.broadcasted_iota(jnp.int32, segment_ids.shape, 1)
    key_ids = jnp.where(positions < lengths[:, None], segment_ids, -1)
    seq_ids = lax.dynamic_index_in_dim(key_ids, c // 2, 0, keepdims=False)
    row_ids = jnp.broadcast_to(seq_ids[None, :], (8, all_rows))
    own_ids = lax.dynamic_slice_in_dim(seq_ids, lax.rem(c, 2) * own_rows, own_rows)
    col_ids = jnp.broadcast_to(own_ids[:, None], (own_rows, 128))

    mats = (query_weight, key_weight, value_weight, output_weight, inner_weight, outer_weight)
    vecs = (query_bias, value_bias, output_bias, outer_bias, inner_bias, first_gain, first_shift, second_gain, second_shift)
    if fused:
        vec_in = pack_vectors(*vecs, cols, half)
    else:
        mats = tuple(
            lax.all_gather(mat, "shard", axis=axis, tiled=True) for mat, axis in zip(mats, (1, 1, 1, 2, 1, 2))
        )
        full = [lax.all_gather(vec, "shard", axis=1, tiled=True) for vec in vecs]
        vec_in = jnp.stack(
            [
                pack_vectors(*[vec.reshape(LAYERS, 2, -1)[:, side] for vec in full], cols, half)
                for side in range(2)
            ]
        )

    n_units = 12 * LAYERS
    out_shape = [
        jax.ShapeDtypeStruct((2, part, width), BF16),
        jax.ShapeDtypeStruct((2, part, width), BF16),
        jax.ShapeDtypeStruct((n_units, cols, half) if fused else (2, n_units, cols, half), BF16),
        jax.ShapeDtypeStruct((LAYERS, VEC_ROWS, width), F32),
    ]
    vm = pltpu.VMEM
    dma = pltpu.SemaphoreType.DMA
    scratch = [
        vm((LAYERS, width, cols), BF16),
        vm((LAYERS, width, cols), BF16),
        vm((LAYERS, width, cols), BF16),
        vm((LAYERS, cols, width), BF16),
        vm((LAYERS, width, units), BF16),
        vm((LAYERS, units, width), BF16),
        vm((2, LAYERS, 16, half), F32),
        vm((rows, width), F32),
        vm((rows, width), F32),
        vm((rows, width), F32),
        vm((rows, width), F32),
        vm((rows, width), BF16),
        vm((rows, width), BF16),
        vm((2, part, width), BF16),
        vm((2, part, width), BF16),
        vm((LAYERS, rows, width), F32),
        vm((LAYERS, rows, width), F32),
        vm((LAYERS, rows, 128), F32),
        vm((LAYERS, rows, 128), F32),
        vm((LAYERS, 8, rows, width), BF16),
        vm((LAYERS, own_rows, cols), BF16),
        vm((LAYERS, all_rows, cols), BF16),
        vm((LAYERS, all_rows, cols), BF16),
        vm((LAYERS, own_rows, cols), BF16),
        vm((LAYERS, 4, rows, width), BF16),
        vm((LAYERS, own_rows, units), BF16),
        vm((LAYERS, own_rows, units), BF16),
        vm((LAYERS, 3, own_rows, all_rows), BF16),
        vm((4, rows, width), BF16),
        vm((4, rows, width), BF16),
        vm((own_rows, units), BF16),
        vm((own_rows, cols), BF16),
        vm((own_rows, cols), BF16),
        vm((all_rows, cols), BF16),
        vm((all_rows, cols), BF16),
        vm((all_rows, cols), F32),
        vm((all_rows, cols), F32),
        vm((8, rows, width), F32),
        vm((2, 3, rows, width), BF16),
        vm((5, 3, rows, width), BF16),
        vm((rows, width), BF16),
        vm((LAYERS, rows, width), BF16),
        vm((n_units, cols, half), BF16),
        vm((12, cols, half), BF16),
        vm((n_units, cols, half), BF16),
        vm((n_units, cols, half), BF16),
        vm((n_units, cols, half), BF16),
        dma((LAYERS, 7)),
        dma((LAYERS, 7)),
        dma((LAYERS, 7)),
        dma((4, 2)),
        dma((4, 2)),
        dma((LAYERS, 7)),
        dma((LAYERS, 7)),
        dma((LAYERS, 3, 3)),
        dma((LAYERS, 3, 3)),
        dma((5, 3)),
        dma((5, 3)),
        dma((LAYERS,)),
        dma((LAYERS,)),
        dma((n_units,)),
        dma((n_units,)),
        dma((n_units,)),
        dma((n_units,)),
        dma((n_units,)),
        dma((n_units,)),
        dma((n_units,)),
        dma((n_units,)),
        dma((n_units,)),
    ]
    vmem = pl.BlockSpec(memory_space=pltpu.VMEM)
    hbm = pl.BlockSpec(memory_space=pl.ANY)
    layer_out, grad_tokens, grad_mats, grad_vecs = pl.pallas_call(
        functools.partial(step_kernel, (width, cols, units, half), fused),
        out_shape=out_shape,
        in_specs=[vmem] * 5 + [hbm] * 6,
        out_specs=[vmem, vmem, hbm, vmem],
        scratch_shapes=scratch,
        compiler_params=pltpu.CompilerParams(
            collective_id=0, has_side_effects=True, vmem_limit_bytes=67043328
        ),
        name="encoder_step",
    )(tokens, cotangent, col_ids, row_ids, vec_in, *mats)

    if not fused:
        both = jnp.concatenate([grad_mats[0], grad_mats[1]], axis=-1)
        both = lax.psum_scatter(both, "shard", scatter_dimension=2, tiled=True)
        grad_mats = lax.psum(both, "ctx")
    keep = grad_mats.shape[-1]
    units_of = grad_mats.reshape(LAYERS, 12, cols, keep)[::-1]

    def flip(block):
        return jnp.swapaxes(block, 1, 2).astype(F32)

    grad_outer = units_of[:, 0:4].reshape(LAYERS, units, keep).astype(F32)
    grad_inner = flip(units_of[:, 4:8].reshape(LAYERS, units, keep))
    grad_output = units_of[:, 8].astype(F32)
    grad_query, grad_key, grad_value = (flip(units_of[:, 9 + at]) for at in range(3))

    total = lax.psum(grad_vecs, ("shard", "ctx", "tp"))
    at = lax.axis_index("shard")

    def owned(vec):
        count = vec.shape[1] // shards
        return lax.dynamic_slice_in_dim(vec, at * count, count, 1)

    vec_query = owned(total[:, 6:10, :cols].reshape(LAYERS, -1))
    vec_value = owned(total[:, 10:14, :cols].reshape(LAYERS, -1))
    vec_inner = owned(total[:, 14:18].reshape(LAYERS, -1))
    vec_outer, vec_output, gain_one, shift_one, gain_two, shift_two = (owned(total[:, row]) for row in range(6))
    return (
        layer_out,
        grad_tokens.astype(F32),
        grad_query,
        grad_key,
        grad_value,
        grad_output,
        grad_inner,
        grad_outer,
        vec_query,
        vec_value,
        vec_output,
        vec_inner,
        vec_outer,
        gain_one,
        shift_one,
        gain_two,
        shift_two,
    )


def solution(mesh):
    rows = P("shard", ("ctx", "tp"), None)
    down = P(None, "shard", "tp")
    across = P(None, "tp", "shard")
    vector = P(None, "shard")
    mats = (down, down, down, across, down, across)
    return jax.shard_map(
        per_device,
        mesh=mesh,
        in_specs=(rows, rows, P("shard", None), P("shard")) + mats + (vector,) * 9,
        out_specs=(rows, rows) + mats + (vector,) * 9,
        check_vma=False,
    )
```

time: 969 us -> 509 us (0.53)
  Pallas kernels: 0 us -> 348 us
  waiting for transfers between devices: 449 us -> 109 us
  blocking collectives: 271 us -> 0 us
  matrix products: 99.4 us -> 0 us
  other arithmetic: 50.8 us -> 6.32 us
  local copies, waits for them, and re-layouts: 68.3 us -> 28.6 us
    pallas_call x0 -> x1, Pallas kernels: none -> 348 us  [per_device(): pl.pallas_call(functools.partial(step_kernel, (width, cols, units, half),...]
    all_gather x38 -> x0, blocking collectives: 271 us -> none  [the longest x8 65.6 us: rows_all(): return lax.all_gather(local_rows, 'tp', axis=1, tiled=True)]
    reduce_scatter x14 -> x0, waiting for transfers between devices: 180 us -> none  [the longest x8 91.1 us: rows_sum(): lax.psum_scatter(partial_rows.astype(jnp.bfloat16), 'tp', scatter_dimensi...]
    unnamed x40 -> x1, waiting for transfers between devices: 146 us -> 0.02 us
    dot_general x46 -> x0, matrix products: 88.2 us -> none  [the longest x2 9.19 us: layer_backward(): jnp.einsum('shqk,sqhd->skhd', probs_low, grad_mixed, preferred_element_ty...]
    unnamed x254 -> x29, local copies, waits for them, and re-layouts: 43 us -> 11.9 us
    reduce_sum x22 -> x0, other arithmetic: 20.5 us -> none  [the longest x8 9.31 us: layer_norm(): center = resid - jnp.mean(resid, axis=-1, keepdims=True)]
    all_gather x4 -> x0, waiting for transfers between devices: 15.3 us -> none  [the longest x2 15.3 us: fetch(): lax.all_gather(outer_weight[layer_at], 'shard', axis=1, tiled=True)]
  transfers between devices with their start and end apart: 30 -> 1, of which waited for: 24 -> 1; matrix products, arithmetic and copies ran while one was open for 13% -> 2% of each run, Pallas kernels for 0% -> 0%
where the time goes in v1:
time: 509 us; the launch traced here: 506 us
  Pallas kernels  348 us (68%)
  waiting for transfers between devices  109 us (21%)
  local copies, waits for them, and re-layouts  28.6 us (6%)
  between operations  14.2 us (3%)
  other arithmetic  6.32 us (1%)
    pallas_call x1, Pallas kernels, per_device(): pl.pallas_call(functools.partial(step_kernel, (width, cols, units, half),...  348 us
    psum x1, waiting for transfers between devices, per_device(): total = lax.psum(grad_vecs, ('shard', 'ctx', 'tp'))  109 us
    unnamed x29, local copies, waits for them, and re-layouts  11.9 us
  transfers between devices with their start and end apart: 1, of which 1 were waited for; matrix products, arithmetic and copies ran while one was open for 2% of the time, Pallas kernels for 0%

profile of v1, /device:TPU:0, one launch (start us, length us, event | category | flops | bytes accessed | tf_op | source)
XLA Modules:
  0.0 506.5 jit_solution(1955317166376044785)
XLA Ops:
  7.2 0.0 all-reduce.5.cloned.1.call-start
  7.3 0.8 compare_select_fusion
  8.1 0.8 reshape.106
  8.9 0.8 reshape.107
  9.6 0.7 copy.44
  10.3 0.7 copy.45
  11.0 0.7 copy.46
  11.7 0.7 copy.47
  12.4 0.7 copy.48
  13.1 0.7 copy.49
  13.7 0.7 reshape.114
  14.4 0.1 concatenate.4
  14.5 0.6 pad_convert_fusion.refs_4_
  15.2 1.9 copy.50.refs_5_
  17.0 1.9 copy.51.refs_6_
  18.9 0.9 copy.52.refs_7_
  19.8 0.1 dynamic_slice.46
  19.9 0.8 broadcast_in_dim.23.refs_2_
  20.8 0.6 broadcast_in_dim.25.refs_3_
  21.4 348.2 %encoder_step.1 = (bf16[2,64,768]{2,1,0:T(8,128)(2,1)}, bf16[2,64,768]{2,1,0:T(8,128)(2,1)}, bf16[24,192,384]{2,1,0:T(8,128)(2,1)}, f32[2,24,768]{2,1,0:T(8,128)}) custom-call(bf16[2,64,768]{2,1,0:T(8,128)(2,1)} %refs_0_.1, bf16[2,64,768]{2,1,0:T(8,128)(2,1)} %refs_1_.1, s32[512,128]{1,0:T(8,128)} %broadcast_in_dim.23.refs_2_, ...), custom_call_target="tpu_custom_call" | custom-call | tf_op jit(solution)/shard_map/encoder_step/pallas_call | solution.py:926
  369.6 0.0 all-reduce.5.cloned.1.call-update
  369.6 2.3 fusion.1
  371.9 3.0 fusion
  374.9 0.8 convert_element_type.65
  375.6 0.1 slice.72
  375.8 0.3 convert_bitcast_fusion
  376.0 0.0 copy-start
  376.0 2.0 copy.53
  378.0 0.1 slice.74
  378.2 1.7 bitcast_convert_fusion
  379.8 1.1 convert_bitcast_fusion.3
  380.9 0.1 copy-done.2
  381.0 1.1 convert_bitcast_fusion.1
  382.1 109.1 %all-reduce.5.cloned.1.call-done = f32[2,24,768]{2,1,0:T(8,128)} async-done(((f32[2,24,768]{2,1,0:T(8,128)}), f32[2,24,768]{2,1,0:T(8,128)}) %all-reduce.5.cloned.1.call-update) | async-done | bytes 147472 | tf_op jit(solution)/shard_map/psum | solution.py:953
  491.2 0.8 fusion.3
  492.1 0.1 reshape.117
  492.1 0.1 reshape.116
  492.2 1.1 fusion.2
  493.4 0.6 copy.72
  493.9 0.9 slice_bitcast_fusion
  494.9 0.6 copy.71
  495.4 0.6 copy.70
  496.0 0.6 copy.69
  496.6 0.6 copy.68
  497.2 0.6 copy.67
  497.8 0.6 constant_dynamic-slice_fusion.7
  498.4 0.6 constant_dynamic-slice_fusion.5
  499.0 0.7 copy.75
  (21 shorter events, 0.1 us)
Async XLA Ops:
  7.2 11.7 %copy-start.5 = (bf16[2,384,192]{1,2,0:T(8,128)(2,1)S(1)}, bf16[2,384,192]{1,2,0:T(8,128)(2,1)}, u32[]{:S(2)}) copy-start(bf16[2,384,192]{1,2,0:T(8,128)(2,1)} %param.25) | copy-start | bytes 884740
  7.2 484.0 %all-reduce.5.cloned.1.call-start = ((), (), s32[]{:S(2)}) async-start(), calls=%async_computation | async-start | bytes 294912 | tf_op jit(solution)/shard_map/psum | solution.py:953
  371.9 3.0 copy-start.7
  376.0 2.0 copy-start
  378.1 1.7 copy-start.3
  378.1 1.7 copy-start.4
  379.8 1.1 copy-start.1
  379.8 1.2 copy-start.2
  380.9 118.0 %copy-start.6 = (bf16[2,64,768]{2,1,0:T(8,128)(2,1)S(1)}, bf16[2,64,768]{2,1,0:T(8,128)(2,1)}, u32[]{:S(2)}) copy-start(bf16[2,64,768]{2,1,0:T(8,128)(2,1)} %get-tuple-element.85) | copy-start | bytes 589828
Sparse Core Ops, SparseCore 0:
  369.7 121.4 all-reduce.4

commit v2 on v1

--- a/solution.py
+++ b/solution.py
@@ -15,6 +15,7 @@
 BF16 = jnp.bfloat16
 NEG = -1e30
 VEC_ROWS = 24
+LAGS = (4, 6, 8, 10)
 
 
 def nn(a, b):
@@ -48,9 +49,9 @@
     (
         tok_ref,
         cot_ref,
-        idc_ref,
-        idr_ref,
-        vec_ref,
+        seg_ref,
+        vec_refs,
+        len_ref,
         wq_ref,
         wk_ref,
         wv_ref,
@@ -62,12 +63,12 @@
         out_mat,
         out_vec,
         WQ,
-        WK,
-        WV,
         WO,
         WI,
         WU,
         VB,
+        IDC,
+        IDR,
         H,
         N1,
         DR,
@@ -108,9 +109,15 @@
         XR,
         YR,
         Y2,
+        OV,
+        VR,
         wl_sem,
         ws_sem,
         wr_sem,
+        wz_s,
+        wz_r,
+        v_s,
+        v_r,
         rd_s,
         rd_r,
         g8_s,
@@ -130,7 +137,7 @@
         z3_s,
         z3_r,
         om_sem,
-    ) = refs
+    ) = refs[:3] + (refs[3:12],) + refs[12:]
     width, cols, units, half = dims
     seqs, part = tok_ref.shape[0], tok_ref.shape[1]
     rows = 2 * part
@@ -175,47 +182,114 @@
         pl.semaphore_signal(bar, 1, device_id=(1 - s, c, t), device_id_type=MESH)
     pl.semaphore_wait(bar, 16 if fused else 15)
 
-    row_at = pl.multiple_of(s * half, half)
-
-    def weight_views(layer):
-        if not fused:
-            return [
-                (wq_ref.at[layer], WQ.at[layer]),
-                (wk_ref.at[layer], WK.at[layer]),
-                (wv_ref.at[layer], WV.at[layer]),
-                (wo_ref.at[layer], WO.at[layer]),
-                (wi_ref.at[layer], WI.at[layer]),
-                (wu_ref.at[layer], WU.at[layer]),
-            ]
-        return [
-            (wq_ref.at[layer], WQ.at[layer, pl.ds(row_at, half)]),
-            (wk_ref.at[layer], WK.at[layer, pl.ds(row_at, half)]),
-            (wv_ref.at[layer], WV.at[layer, pl.ds(row_at, half)]),
-            (wo_ref.at[layer], WO.at[layer, :, pl.ds(row_at, half)]),
-            (wi_ref.at[layer], WI.at[layer, pl.ds(row_at, half)]),
-            (wu_ref.at[layer], WU.at[layer, :, pl.ds(row_at, half)]),
-        ]
-
-    def weight_copies(layer, item):
-        src, dst = weight_views(layer)[item]
-        local = pltpu.make_async_copy(src, dst, wl_sem.at[layer, item])
-        remote = None
+    def unit_view(layer, item, side):
+        at = pl.multiple_of(side * half, half)
+        lanes = pl.ds(at, half)
+        if item < 3:
+            return WQ.at[layer, pl.ds(item * cols, cols), lanes]
+        if item == 3:
+            return WO.at[layer, :, lanes]
+        if item < 8:
+            return WI.at[layer, pl.ds(at + (item - 4) * (half // 4), half // 4)]
+        return WU.at[layer, pl.ds((item - 8) * cols, cols), lanes]
+
+    def unit_arg(layer, item):
+        if item < 4:
+            return (wq_ref, wk_ref, wv_ref, wo_ref)[item].at[layer]
+        if item < 8:
+            return wi_ref.at[layer, pl.ds((item - 4) * (half // 4), half // 4)]
+        return wu_ref.at[layer, pl.ds((item - 8) * cols, cols)]
+
+    def local_copy(layer, item):
+        lanes = pl.ds(pl.multiple_of(s * half, half), half) if fused else pl.ds(0, width)
+        if item < 3:
+            src, dst = (wq_ref, wk_ref, wv_ref)[item], WQ.at[layer, pl.ds(item * cols, cols), lanes]
+        elif item == 3:
+            src, dst = wo_ref, WO.at[layer, :, lanes]
+        elif item == 4:
+            src, dst = wi_ref, WI.at[layer, lanes]
+        else:
+            src, dst = wu_ref, WU.at[layer, :, lanes]
+        return pltpu.make_async_copy(src.at[layer], dst, wl_sem.at[layer, item])
+
+    def over_x(layer, item):
+        return rc(
+            unit_arg(layer, item),
+            unit_view(layer, item, s),
+            ws_sem.at[layer, item],
+            wr_sem.at[layer, item],
+            c,
+            t,
+            1 - s,
+        )
+
+    def over_z(layer, item):
+        view = unit_view(layer, item, 1 - s)
+        return rc(view, view, wz_s.at[layer, item], wz_r.at[layer, item], zp, t)
+
+    def direct(layer, item):
+        return jnp.logical_and(layer == 0, item < 4)
+
+    def mine_over_x(layer, item):
+        return jnp.logical_or(direct(layer, item), hf == item % 2)
+
+    def fetch_start(layer, item):
+        @pl.when(mine_over_x(layer, item))
+        def _():
+            over_x(layer, item).start()
+
+    def fetch_pass(layer, items):
         if fused:
-            remote = rc(src, dst, ws_sem.at[layer, item], wr_sem.at[layer, item], c, t, 1 - s)
-        return local, remote
-
-    def weight_wait(layer, item):
-        local, remote = weight_copies(layer, item)
-        local.wait()
-        if fused:
-            remote.wait()
+            for item in items:
+
+                @pl.when(hf == item % 2)
+                def _():
+                    over_x(layer, item).wait_recv()
+                    over_z(layer, item).start()
+
+    def fetch_wait(layer, items):
+        for item in items:
+            local_copy(layer, {0: 0, 1: 1, 2: 2, 3: 3, 4: 4, 8: 5}[item]).wait() if item in (0, 1, 2, 3, 4, 8) else None
+            if fused:
+
+                @pl.when(direct(layer, item))
+                def _():
+                    over_x(layer, item).wait_recv()
+
+                @pl.when(jnp.logical_not(mine_over_x(layer, item)))
+                def _():
+                    over_z(layer, item).wait_recv()
+
+    def fetch_drain(layer):
+        for item in range(12):
+
+            @pl.when(mine_over_x(layer, item))
+            def _():
+                over_x(layer, item).wait_send()
+
+            @pl.when(jnp.logical_and(hf == item % 2, jnp.logical_not(direct(layer, item))))
+            def _():
+                over_z(layer, item).wait_send()
+
+    def fill_vectors(side, at):
+        for layer in range(LAYERS):
+            for place, ref in ((0, vec_refs[0]), (2, vec_refs[1])):
+                value = ref[...].astype(F32)[layer : layer + 1, at : at + half]
+                VB[side, layer, place : place + 1, :cols] = value[:, :cols]
+                VB[side, layer, place + 1 : place + 2, :cols] = value[:, cols:]
+            for place, ref in zip((4, 5, 6, 7, 8, 9), vec_refs[2:4] + vec_refs[5:9]):
+                VB[side, layer, place : place + 1] = ref[...].astype(F32)[layer : layer + 1, at : at + half]
+            value = vec_refs[4][...].astype(F32)[layer : layer + 1, 4 * at : 4 * at + 4 * half]
+            for j in range(4):
+                VB[side, layer, 10 + j : 11 + j] = value[:, j * half : (j + 1) * half]
 
     if fused:
-        vec_copy = rc(vec_ref, VB.at[s], ws_sem.at[0, 6], wr_sem.at[0, 6], c, t, 1 - s)
+        fill_vectors(s, 0)
+        vec_copy = rc(VB.at[s], VB.at[s], ws_sem.at[0, 12], wr_sem.at[0, 12], c, t, 1 - s)
         vec_copy.start()
-        VB[s] = vec_ref[...]
     else:
-        VB[...] = vec_ref[...]
+        fill_vectors(0, 0)
+        fill_vectors(1, half)
 
     b_me = c // 2
     spread_t = 2 * hf + y
@@ -318,12 +392,19 @@
 
     spread_start(tok_ref, TK, 0)
     for layer in range(LAYERS):
+        if fused:
+            for item in range(12):
+                fetch_start(layer, item)
         for item in range(6):
-            local, remote = weight_copies(layer, item)
-            local.start()
-            if fused:
-                remote.start()
+            local_copy(layer, item).start()
     spread_start(cot_ref, CO, 1)
+
+    ids = seg_ref[pl.ds(b_me, 1)]
+    places = lax.broadcasted_iota(jnp.int32, ids.shape, 1)
+    ids = jnp.where(places < len_ref[b_me], ids, -1).astype(F32)
+    IDR[...] = jnp.broadcast_to(ids, IDR.shape)
+    own_ids = jnp.where(hf == 0, ids[:, :own_rows], ids[:, own_rows:])
+    IDC[...] = jnp.broadcast_to(own_ids, (128, own_rows)).T
 
     def gather_copies(buf, ssem, rsem):
         return (
@@ -377,10 +458,10 @@
     def vec_at(layer, row, lanes):
         return VB[y, layer, pl.ds(row, 1)][:, :lanes]
 
-    out_vec[...] = jnp.zeros_like(out_vec)
+    OV[...] = jnp.zeros_like(OV)
 
     def put_vec(layer, row, value):
-        out_vec[layer, pl.ds(row, 1), : value.shape[1]] = value
+        OV[layer, pl.ds(row, 1), : value.shape[1]] = value
 
     if fused:
         vec_copy.wait()
@@ -415,8 +496,7 @@
         to_y.start()
         to_z.start()
         to_c.start()
-        for item in range(3):
-            weight_wait(layer, item)
+        fetch_wait(layer, (0, 1, 2))
 
         def project(at, with_q):
             block = XB[layer, pl.ds(at, 2)].reshape(2 * rows, width)
@@ -424,10 +504,10 @@
             if with_q:
                 mine = pl.ds(pl.multiple_of((at - own) * rows, 2 * rows), 2 * rows)
                 qb = vec_at(layer, k, cols)
-                q_low = (nn(block, WQ[layer]) + qb).astype(BF16)
+                q_low = (nt(block, WQ[layer, :cols]) + qb).astype(BF16)
                 Q[layer, mine] = q_low * jnp.asarray(HD**-0.5, BF16)
-            K[layer, where] = nn(block, WK[layer]).astype(BF16)
-            V[layer, where] = (nn(block, WV[layer]) + vec_at(layer, 2 + k, cols)).astype(BF16)
+            K[layer, where] = nt(block, WQ[layer, cols : 2 * cols]).astype(BF16)
+            V[layer, where] = (nt(block, WQ[layer, 2 * cols :]) + vec_at(layer, 2 + k, cols)).astype(BF16)
 
         to_c.wait_recv()
         project(own + 2 * y, True)
@@ -449,7 +529,7 @@
 
         def attend(at, inner):
             where = pl.ds(pl.multiple_of(at * tile, tile), tile)
-            ids = idc_ref[where][:, :1] == idr_ref[:1]
+            ids = IDC[where][:, :1] == IDR[:1]
             q_tile = Q[layer, where]
             mixed = []
             for head in range(3):
@@ -465,7 +545,7 @@
             return inner
 
         lax.fori_loop(0, 2, attend, 0)
-        weight_wait(layer, 3)
+        fetch_wait(layer, (3,))
 
         def project_out(at):
             where = pl.ds(pl.multiple_of(at * 2 * rows, 2 * rows), 2 * rows)
@@ -476,6 +556,7 @@
         sum_remote(copies, PF, 0, 0)
         project_out(y)
         sum_local(copies, PF, 0, 0)
+        fetch_pass(layer, (4, 5, 6, 7))
         branch = sum_finish(copies, PF, 0, 0) + full_vec(layer, 4)
         normed, xhat, rstd = norm_forward(H[...] + branch, full_vec(layer, 6), full_vec(layer, 7))
         N1[...] = normed
@@ -485,8 +566,8 @@
         N1B[layer, t] = normed.astype(BF16)
         moves = gather_copies(N1B.at[layer], g4_s.at[layer, 0], g4_r.at[layer, 0])
         gather_start(moves)
-        weight_wait(layer, 4)
-        weight_wait(layer, 5)
+        fetch_pass(layer, (8, 9, 10, 11))
+        fetch_wait(layer, (4, 5, 6, 7))
 
         def feed(at):
             where = pl.ds(pl.multiple_of(at * 2 * rows, 2 * rows), 2 * rows)
@@ -502,12 +583,18 @@
 
         copies = sum_copies(1, 0)
         moves[0].wait_recv()
+        fetch_wait(layer, (8, 9, 10, 11))
         feed(y)
         sum_local(copies, PF, 1, 0)
         gather_remote(moves)
         feed(1 - y)
         sum_remote(copies, PF, 1, 0)
         gather_finish(moves)
+
+        @pl.when(layer == 0)
+        def _():
+            fetch_pass(1, (0, 1, 2, 3))
+
         second = N1[...] + sum_finish(copies, PF, 1, 0) + full_vec(layer, 5)
         result, xhat, rstd = norm_forward(second, full_vec(layer, 8), full_vec(layer, 9))
         XH2[layer] = xhat
@@ -515,31 +602,141 @@
         H[...] = result
         return carry
 
-    for layer in range(LAYERS):
-        forward_layer(layer, 0)
+    lax.fori_loop(0, LAYERS, forward_layer, 0)
 
     TK[...] = H[...].astype(BF16)
     collect_start(TK, OT, 2)
     spread_wait(cot_ref, CO, 1)
     H[...] = CO[...].astype(F32)
 
-    first_half = row_at if fused else 0
-    other_half = pl.multiple_of((1 - s) * half, half) if fused else half
-
-    def split_grad(a, b_ref_at, unit, step, count):
-        for own_side in (True, False):
-            at = first_half if own_side else other_half
-            value = tn(a, b_ref_at(at)).astype(BF16)
-            value = value.reshape(count, cols, half)
-            if own_side:
-                GO[pl.ds(unit, count)] = value
-            elif fused:
-                GS[pl.ds(step, count)] = value
-            else:
-                XR[pl.ds(unit, count)] = value
-
-    def backward_layer(layer):
-        base = (LAYERS - 1 - layer) * 12
+    total_units = 12 * LAYERS
+
+    def x_copy(unit):
+        return rc(GS.at[lax.rem(unit, 12)], XR.at[unit], xs_s.at[unit], xs_r.at[unit], c, t, 1 - s)
+
+    def z1_copy(unit):
+        return rc(GO.at[unit], YR.at[unit], z1_s.at[unit], z1_r.at[unit], z_in, t)
+
+    def z2_copy(unit):
+        return rc(GO.at[unit], Y2.at[unit], z2_s.at[unit], z2_r.at[unit], z_mid, t)
+
+    def z3_copy(unit):
+        return rc(GO.at[unit], YR.at[unit], z3_s.at[unit], z3_r.at[unit], z_out, t)
+
+    def add_into(unit, other):
+        GO[unit] = (GO[unit].astype(F32) + other.astype(F32)).astype(BF16)
+
+    def stage_z1(unit):
+        x_copy(unit).wait()
+        add_into(unit, XR[unit])
+
+        @pl.when(is_outer)
+        def _():
+            z1_copy(unit).start()
+
+    def stage_z2(unit):
+        @pl.when(is_inner)
+        def _():
+            z1_copy(unit).wait_recv()
+            add_into(unit, YR[unit])
+            z2_copy(unit).start()
+
+        @pl.when(is_outer)
+        def _():
+            z1_copy(unit).wait_send()
+
+    def stage_z3(unit):
+        @pl.when(is_inner)
+        def _():
+            z2_copy(unit).wait()
+            add_into(unit, Y2[unit])
+            z3_copy(unit).start()
+
+    def stage_out(unit):
+        @pl.when(is_inner)
+        def _():
+            z3_copy(unit).wait_send()
+            pltpu.make_async_copy(GO.at[unit], out_mat.at[unit], om_sem.at[unit]).start()
+
+        @pl.when(is_outer)
+        def _():
+            z3_copy(unit).wait_recv()
+            pltpu.make_async_copy(YR.at[unit], out_mat.at[unit], om_sem.at[unit]).start()
+
+    stages = ((stage_out, LAGS[3]), (stage_z3, LAGS[2]), (stage_z2, LAGS[1]), (stage_z1, LAGS[0]))
+
+    def advance(tick):
+        for stage, lag in stages:
+            unit = tick - lag
+
+            @pl.when(jnp.logical_and(unit >= 0, unit < total_units))
+            def _(stage=stage, unit=unit):
+                stage(unit)
+
+    def vec_step(layer, at):
+        partner = (
+            (s, c, tc),
+            (s, c, ty),
+            (1 - s, c, t),
+            (s, zp, t),
+            (s, lax.rem(c + 2, 4), t),
+        )[at]
+        return pltpu.make_async_remote_copy(
+            src_ref=OV.at[layer],
+            dst_ref=VR.at[layer, at],
+            send_sem=v_s.at[layer, at],
+            recv_sem=v_r.at[layer, at],
+            device_id=partner,
+            device_id_type=MESH,
+        )
+
+    def vec_move(layer, at):
+        if fused:
+            if at > 0:
+                vec_step(layer, at - 1).wait()
+                OV[layer] += VR[layer, at - 1]
+            if at < 5:
+                vec_step(layer, at).start()
+
+    def side_of(own_side):
+        if fused:
+            return pl.multiple_of((s if own_side else 1 - s) * half, half)
+        return 0 if own_side else half
+
+    def put_units(own_side, base, step, count, value):
+        value = value.astype(BF16).reshape(count, cols, half)
+        if own_side:
+            GO[pl.ds(base + step, count)] = value
+        elif fused:
+            GS[pl.ds(step, count)] = value
+        else:
+            XR[pl.ds(base + step, count)] = value
+
+    def send_units(base, step, count):
+        if fused:
+            for i in range(step, step + count):
+                x_copy(base + i).start()
+
+    def split_grad(a, b_ref_at, base, step, count):
+        for own_side in (False, True):
+            put_units(own_side, base, step, count, tn(a, b_ref_at(side_of(own_side))))
+            if not own_side:
+                send_units(base, step, count)
+
+    def backward_layer(turn, carry):
+        layer = LAYERS - 1 - turn
+        base = turn * 12
+
+        def tick(*places):
+            if fused:
+                for i in places:
+                    advance(base + i)
+
+        def late_vec(at):
+            @pl.when(turn > 0)
+            def _():
+                vec_move(LAYERS - 1, at)
+
         grad = H[...]
         xhat = XH2[layer]
         rstd = SD2[layer][:, :1]
@@ -563,6 +760,8 @@
         moves[0].wait_recv()
         back_feed(y)
         sum_local(copies, PF, 2, 0)
+        tick(0, 1)
+        late_vec(0)
         gather_remote(moves)
         back_feed(1 - y)
         sum_remote(copies, PF, 2, 0)
@@ -572,7 +771,15 @@
             return lambda at: ref[:, :, pl.ds(at, half)].reshape(-1, half)
 
         split_grad(G[layer], halves(DF), base, 0, 4)
-        split_grad(DU[...], halves(N1B.at[layer]), base + 4, 4, 4)
+        tick(2)
+        for own_side in (False, True):
+            left = N1B[layer, :, :, pl.ds(side_of(own_side), half)].reshape(own_rows, half)
+            for at in range(2):
+                put_units(own_side, base, 4 + 2 * at, 2, tn(left, DU[:, at * half : (at + 1) * half]))
+            if not own_side:
+                send_units(base, 4, 4)
+        tick(3)
+        late_vec(1)
         only = jnp.where(t == 0, 1.0, 0.0)
         put_vec(layer, 0, only * jnp.sum(DF[...].reshape(own_rows, width).astype(F32), axis=0, keepdims=True))
         put_vec(layer, 14 + t, jnp.sum(DU[...].astype(F32), axis=0, keepdims=True))
@@ -594,10 +801,12 @@
 
         moves[0].wait_recv()
         back_out(y)
+        tick(4, 5)
+        late_vec(2)
         gather_remote(moves)
         back_out(1 - y)
         gather_finish(moves)
-        split_grad(OB[layer], halves(DA), base + 8, 8, 1)
+        split_grad(OB[layer], halves(DA), base, 8, 1)
         put_vec(layer, 1, only * jnp.sum(DA[...].reshape(own_rows, width).astype(F32), axis=0, keepdims=True))
 
         DKF[...] = jnp.zeros_like(DKF)
@@ -624,7 +833,10 @@
             DQ[where, 2 * HD :] = (d_query[2] * scale).astype(BF16)
             return inner
 
+        tick(6)
         lax.fori_loop(0, 2, back_attend, 0)
+        tick(7, 8)
+        late_vec(3)
         DK[...] = DKF[...].astype(BF16)
         DV[...] = DVF[...].astype(BF16)
         own = hf * 4
@@ -632,10 +844,10 @@
 
         def back_in(at, with_q):
             where = pl.ds(pl.multiple_of(at * rows, 2 * rows), 2 * rows)
-            total = nt(DK[where], WK[layer]) + nt(DV[where], WV[layer])
+            total = nn(DK[where], WQ[layer, cols : 2 * cols]) + nn(DV[where], WQ[layer, 2 * cols :])
             if with_q:
                 mine = pl.ds(pl.multiple_of((at - own) * rows, 2 * rows), 2 * rows)
-                total = total + nt(DQ[mine], WQ[layer])
+                total = total + nn(DQ[mine], WQ[layer, :cols])
             PF[pl.ds(at, 2)] = total.reshape(2, rows, width)
 
         pf_far = PF.at[pl.ds(far, 4)]
@@ -653,111 +865,47 @@
         ZS[...] = sum_finish(far_copies, pf_far, 3, 1).astype(BF16)
         across = rc(ZS, ZR.at[layer], rz_s.at[layer], rz_r.at[layer], zp, t)
         across.start()
+        tick(9)
+        late_vec(4)
 
         def block_cols(ref, start, count):
             return lambda at: ref[pl.ds(start, count), :, pl.ds(at, half)].reshape(-1, half)
 
         xb = XB.at[layer]
-        split_grad(DQ[...], block_cols(xb, own, 4), base + 9, 9, 1)
-        split_grad(DK[...], block_cols(xb, 0, 8), base + 10, 10, 1)
-        split_grad(DV[...], block_cols(xb, 0, 8), base + 11, 11, 1)
+        split_grad(DQ[...], block_cols(xb, own, 4), base, 9, 1)
+        split_grad(DK[...], block_cols(xb, 0, 8), base, 10, 1)
+        split_grad(DV[...], block_cols(xb, 0, 8), base, 11, 1)
+        tick(10)
         put_vec(layer, 6 + t, jnp.sum(DQ[...].astype(F32), axis=0, keepdims=True))
         put_vec(layer, 10 + t, jnp.sum(DV[...].astype(F32), axis=0, keepdims=True))
 
         near = sum_finish(copies, pf_own, 4, 0)
+        tick(11)
+        late_vec(5)
         across.wait()
         H[...] = DR1[...] + near + ZR[layer].astype(F32)
-
-    def x_copy(unit, step):
-        return rc(GS.at[step], XR.at[unit], xs_s.at[unit], xs_r.at[unit], c, t, 1 - s)
-
-    def z1_copy(unit):
-        return rc(GO.at[unit], YR.at[unit], z1_s.at[unit], z1_r.at[unit], z_in, t)
-
-    def z2_copy(unit):
-        return rc(GO.at[unit], Y2.at[unit], z2_s.at[unit], z2_r.at[unit], z_mid, t)
-
-    def z3_copy(unit):
-        return rc(GO.at[unit], YR.at[unit], z3_s.at[unit], z3_r.at[unit], z_out, t)
-
-    def add_into(unit, other):
-        GO[unit] = (GO[unit].astype(F32) + other.astype(F32)).astype(BF16)
-
-    def stage_x(unit, step):
-        x_copy(unit, step).start()
-
-    def stage_z1(unit, step):
-        copy = x_copy(unit, step)
-        copy.wait()
-        add_into(unit, XR[unit])
-
-        @pl.when(is_outer)
-        def _():
-            z1_copy(unit).start()
-
-    def stage_z2(unit):
-        @pl.when(is_inner)
-        def _():
-            z1_copy(unit).wait_recv()
-            add_into(unit, YR[unit])
-            z2_copy(unit).start()
-
-        @pl.when(is_outer)
-        def _():
-            z1_copy(unit).wait_send()
-
-    def stage_z3(unit):
-        @pl.when(is_inner)
-        def _():
-            z2_copy(unit).wait()
-            add_into(unit, Y2[unit])
-            z3_copy(unit).start()
-
-    def stage_out(unit):
-        @pl.when(is_inner)
-        def _():
-            z3_copy(unit).wait_send()
-            pltpu.make_async_copy(GO.at[unit], out_mat.at[unit], om_sem.at[unit]).start()
-
-        @pl.when(is_outer)
-        def _():
-            z3_copy(unit).wait_recv()
-            pltpu.make_async_copy(YR.at[unit], out_mat.at[unit], om_sem.at[unit]).start()
-
-    for layer in reversed(range(LAYERS)):
-        backward_layer(layer)
-        if fused:
-            base = (LAYERS - 1 - layer) * 12
-
-            def x_all(i, carry):
-                stage_x(base + i, i)
-                return carry
-
-            def z1_all(i, carry):
-                stage_z1(base + i, i)
-                return carry
-
-            lax.fori_loop(0, 12, x_all, 0)
-            lax.fori_loop(0, 12, z1_all, 0)
-
-    TK2 = CO
-    TK2[...] = H[...].astype(BF16)
-    collect_start(TK2, OG, 3)
-    total_units = 12 * LAYERS
+        return carry
+
+    lax.fori_loop(0, LAYERS, backward_layer, 0)
+    CO[...] = H[...].astype(BF16)
+    collect_start(CO, OG, 3)
+    vec_move(0, 0)
     if fused:
-        for stage in (stage_z2, stage_z3, stage_out):
-
-            def run(i, carry, stage=stage):
-                stage(i)
-                return carry
-
-            lax.fori_loop(0, total_units, run, 0)
+        more = LAGS[3]
+        spots = [0, more // 5, 2 * more // 5, 3 * more // 5, 4 * more // 5]
+        for i in range(more):
+            if i in spots[1:]:
+                vec_move(0, spots.index(i))
+            advance(total_units + i)
+        vec_move(0, 5)
 
         def drain(i, carry):
             pltpu.make_async_copy(GO.at[i], out_mat.at[i], om_sem.at[i]).wait()
             return carry
 
         lax.fori_loop(0, total_units, drain, 0)
+        for layer in range(LAYERS):
+            fetch_drain(layer)
     else:
         own_out = pltpu.make_async_copy(GO, out_mat.at[0], om_sem.at[0])
         far_out = pltpu.make_async_copy(XR, out_mat.at[1], om_sem.at[1])
@@ -765,24 +913,44 @@
         far_out.start()
         own_out.wait()
         far_out.wait()
+    out_vec[...] = OV[...]
     collect_wait(TK, OT, 2)
     out_tok[...] = OT[...]
-    collect_wait(TK2, OG, 3)
+    collect_wait(CO, OG, 3)
     out_grad[...] = OG[...]
 
 
-def pack_vectors(qb, vb, ob, ub, ib, g1, s1, g2, s2, cols, half):
-    def narrow(vec):
-        two = vec.astype(F32).reshape(LAYERS, -1, cols)
-        return jnp.pad(two, ((0, 0), (0, 0), (0, half - cols)))
-
-    def wide(vec):
-        return vec.astype(F32).reshape(LAYERS, -1, half)
-
-    packed = jnp.concatenate(
-        [narrow(qb), narrow(vb), wide(ob), wide(ub), wide(g1), wide(s1), wide(g2), wide(s2), wide(ib)], axis=1
-    )
-    return jnp.pad(packed, ((0, 0), (0, 16 - packed.shape[1]), (0, 0)))
+def finish_kernel(dims, *refs):
+    tok_ref, grad_ref, mat_ref, vec_ref = refs[:4]
+    out_tok, out_grad, out_q, out_k, out_v, out_o, out_i, out_u = refs[4:12]
+    vec_q, vec_v, vec_o, vec_i, vec_u, gain_1, shift_1, gain_2, shift_2 = refs[12:]
+    width, cols, units, half = dims
+    layer = pl.program_id(0)
+    s = lax.axis_index("shard")
+
+    @pl.when(layer == 0)
+    def _():
+        out_tok[...] = tok_ref[...]
+        out_grad[...] = grad_ref[...].astype(F32)
+
+    for i in range(4):
+        out_u[0, i * cols : (i + 1) * cols, :] = mat_ref[i].astype(F32)
+        r, cc = i % 2, i // 2
+        out_i[0, r * cols : (r + 1) * cols, cc * half : (cc + 1) * half] = mat_ref[4 + i].astype(F32)
+    out_o[0] = mat_ref[8].astype(F32)
+    out_q[0] = mat_ref[9].astype(F32)
+    out_k[0] = mat_ref[10].astype(F32)
+    out_v[0] = mat_ref[11].astype(F32)
+    line = pl.ds(layer, 1)
+    at = pl.ds(pl.multiple_of(s * half, half), half)
+    for row, ref in ((0, vec_u), (1, vec_o), (2, gain_1), (3, shift_1), (4, gain_2), (5, shift_2)):
+        ref[line, :] = vec_ref[0, row : row + 1, at]
+    for row, ref in ((6, vec_q), (10, vec_v)):
+        first = vec_ref[0, pl.ds(row + 2 * s, 1), :cols]
+        second = vec_ref[0, pl.ds(row + 1 + 2 * s, 1), :cols]
+        ref[line, :] = jnp.concatenate([first, second], axis=1)
+    vec_i[line, :width] = vec_ref[0, pl.ds(14 + 2 * s, 1)]
+    vec_i[line, width:] = vec_ref[0, pl.ds(15 + 2 * s, 1)]
 
 
 def per_device(
@@ -817,29 +985,23 @@
     own_rows, all_rows = 4 * rows, 8 * rows
     assert cols == 3 * HD and segment_ids.shape[1] == all_rows and units == width == 4 * cols
 
-    c = lax.axis_index("ctx")
-    positions = lax.broadcasted_iota(jnp.int32, segment_ids.shape, 1)
-    key_ids = jnp.where(positions < lengths[:, None], segment_ids, -1)
-    seq_ids = lax.dynamic_index_in_dim(key_ids, c // 2, 0, keepdims=False)
-    row_ids = jnp.broadcast_to(seq_ids[None, :], (8, all_rows))
-    own_ids = lax.dynamic_slice_in_dim(seq_ids, lax.rem(c, 2) * own_rows, own_rows)
-    col_ids = jnp.broadcast_to(own_ids[:, None], (own_rows, 128))
-
-    mats = (query_weight, key_weight, value_weight, output_weight, inner_weight, outer_weight)
+    def turned(mat):
+        return jnp.swapaxes(mat, 1, 2)
+
+    mats = (
+        turned(query_weight),
+        turned(key_weight),
+        turned(value_weight),
+        output_weight,
+        inner_weight,
+        outer_weight,
+    )
     vecs = (query_bias, value_bias, output_bias, outer_bias, inner_bias, first_gain, first_shift, second_gain, second_shift)
-    if fused:
-        vec_in = pack_vectors(*vecs, cols, half)
-    else:
+    if not fused:
         mats = tuple(
-            lax.all_gather(mat, "shard", axis=axis, tiled=True) for mat, axis in zip(mats, (1, 1, 1, 2, 1, 2))
+            lax.all_gather(mat, "shard", axis=axis, tiled=True) for mat, axis in zip(mats, (2, 2, 2, 2, 1, 2))
         )
-        full = [lax.all_gather(vec, "shard", axis=1, tiled=True) for vec in vecs]
-        vec_in = jnp.stack(
-            [
-                pack_vectors(*[vec.reshape(LAYERS, 2, -1)[:, side] for vec in full], cols, half)
-                for side in range(2)
-            ]
-        )
+        vecs = tuple(lax.all_gather(vec, "shard", axis=1, tiled=True) for vec in vecs)
 
     n_units = 12 * LAYERS
     out_shape = [
@@ -851,13 +1013,13 @@
     vm = pltpu.VMEM
     dma = pltpu.SemaphoreType.DMA
     scratch = [
-        vm((LAYERS, width, cols), BF16),
-        vm((LAYERS, width, cols), BF16),
-        vm((LAYERS, width, cols), BF16),
+        vm((LAYERS, 3 * cols, width), BF16),
         vm((LAYERS, cols, width), BF16),
         vm((LAYERS, width, units), BF16),
         vm((LAYERS, units, width), BF16),
         vm((2, LAYERS, 16, half), F32),
+        vm((own_rows, 128), F32),
+        vm((8, all_rows), F32),
         vm((rows, width), F32),
         vm((rows, width), F32),
         vm((rows, width), F32),
@@ -898,9 +1060,15 @@
         vm((n_units, cols, half), BF16),
         vm((n_units, cols, half), BF16),
         vm((n_units, cols, half), BF16),
-        dma((LAYERS, 7)),
-        dma((LAYERS, 7)),
-        dma((LAYERS, 7)),
+        vm((LAYERS, VEC_ROWS, width), F32),
+        vm((LAYERS, 5, VEC_ROWS, width), F32),
+        dma((LAYERS, 6)),
+        dma((LAYERS, 13)),
+        dma((LAYERS, 13)),
+        dma((LAYERS, 12)),
+        dma((LAYERS, 12)),
+        dma((LAYERS, 5)),
+        dma((LAYERS, 5)),
         dma((4, 2)),
         dma((4, 2)),
         dma((LAYERS, 7)),
@@ -926,29 +1094,53 @@
     layer_out, grad_tokens, grad_mats, grad_vecs = pl.pallas_call(
         functools.partial(step_kernel, (width, cols, units, half), fused),
         out_shape=out_shape,
-        in_specs=[vmem] * 5 + [hbm] * 6,
+        in_specs=[vmem] * 12 + [pl.BlockSpec(memory_space=pltpu.SMEM)] + [hbm] * 6,
         out_specs=[vmem, vmem, hbm, vmem],
         scratch_shapes=scratch,
         compiler_params=pltpu.CompilerParams(
             collective_id=0, has_side_effects=True, vmem_limit_bytes=67043328
         ),
         name="encoder_step",
-    )(tokens, cotangent, col_ids, row_ids, vec_in, *mats)
-
-    if not fused:
-        both = jnp.concatenate([grad_mats[0], grad_mats[1]], axis=-1)
-        both = lax.psum_scatter(both, "shard", scatter_dimension=2, tiled=True)
-        grad_mats = lax.psum(both, "ctx")
-    keep = grad_mats.shape[-1]
-    units_of = grad_mats.reshape(LAYERS, 12, cols, keep)[::-1]
-
-    def flip(block):
-        return jnp.swapaxes(block, 1, 2).astype(F32)
-
-    grad_outer = units_of[:, 0:4].reshape(LAYERS, units, keep).astype(F32)
-    grad_inner = flip(units_of[:, 4:8].reshape(LAYERS, units, keep))
-    grad_output = units_of[:, 8].astype(F32)
-    grad_query, grad_key, grad_value = (flip(units_of[:, 9 + at]) for at in range(3))
+    )(tokens, cotangent, segment_ids, *vecs, lengths, *mats)
+
+    if fused:
+        dims = (width, cols, units, half)
+        layer_block = lambda *shape: pl.BlockSpec((1,) + shape, lambda i: (i,) + (0,) * len(shape))
+        whole = lambda *shape: pl.BlockSpec(shape, lambda i: (0,) * len(shape))
+        mat_shapes = [(cols, half)] * 4 + [(half, units), (units, half)]
+        vec_lens = (half, half, half, 4 * half, half, half, half, half, half)
+        outs = pl.pallas_call(
+            functools.partial(finish_kernel, dims),
+            grid=(LAYERS,),
+            out_shape=[
+                jax.ShapeDtypeStruct((2, part, width), BF16),
+                jax.ShapeDtypeStruct((2, part, width), F32),
+            ]
+            + [jax.ShapeDtypeStruct((LAYERS,) + shape, F32) for shape in mat_shapes]
+            + [jax.ShapeDtypeStruct((LAYERS, count), F32) for count in vec_lens],
+            in_specs=[
+                whole(2, part, width),
+                whole(2, part, width),
+                pl.BlockSpec((12, cols, half), lambda i: (LAYERS - 1 - i, 0, 0)),
+                layer_block(VEC_ROWS, width),
+            ],
+            out_specs=[whole(2, part, width), whole(2, part, width)]
+            + [layer_block(*shape) for shape in mat_shapes]
+            + [whole(LAYERS, count) for count in vec_lens],
+            name="write_out",
+        )(layer_out, grad_tokens, grad_mats, grad_vecs)
+        return tuple(outs[:2]) + tuple(turned(mat) for mat in outs[2:5]) + tuple(outs[5:])
+
+    mats = grad_mats.reshape(2, LAYERS, 12, cols, half)[:, ::-1]
+    wide = jnp.concatenate([mats[0], mats[1]], axis=-1)
+    wide = jnp.concatenate([wide[:, :4], wide[:, 8:]], axis=1)
+    wide = lax.psum(lax.psum_scatter(wide, "shard", scatter_dimension=3, tiled=True), "ctx").astype(F32)
+    inner = mats[:, :, 4:8].reshape(2, LAYERS, 2, 2, cols, half)
+    inner = jnp.transpose(inner, (1, 0, 3, 4, 2, 5)).reshape(LAYERS, width, units)
+    inner = lax.psum(lax.psum_scatter(inner, "shard", scatter_dimension=1, tiled=True), "ctx").astype(F32)
+    grad_outer = wide[:, :4].reshape(LAYERS, units, -1)
+    grad_output = wide[:, 4]
+    grad_query, grad_key, grad_value = (turned(wide[:, 5 + at]) for at in range(3))
 
     total = lax.psum(grad_vecs, ("shard", "ctx", "tp"))
     at = lax.axis_index("shard")
@@ -968,7 +1160,7 @@
         grad_key,
         grad_value,
         grad_output,
-        grad_inner,
+        inner,
         grad_outer,
         vec_query,
         vec_value,

time: 509 us -> 257 us (0.50)
  waiting for transfers between devices: 109 us -> 0 us
  Pallas kernels: 348 us -> 256 us
  local copies, waits for them, and re-layouts: 28.6 us -> 0 us
  between operations: 14.2 us -> 0.85 us
  other arithmetic: 6.32 us -> 0 us
    psum x1 -> x0, waiting for transfers between devices: 109 us -> none  [per_device(): total = lax.psum(grad_vecs, ('shard', 'ctx', 'tp'))]
    pallas_call x1, Pallas kernels: 348 us -> 252 us  [per_device(): pl.pallas_call(functools.partial(step_kernel, (width, cols, units, half),...]
    unnamed x29 -> x0, local copies, waits for them, and re-layouts: 11.9 us -> none
    slice x6 -> x0, local copies, waits for them, and re-layouts: 7.42 us -> none  [the longest x2 3.08 us: per_device(): grad_outer = units_of[:, 0:4].reshape(LAYERS, units, keep).astype(F32)]
    reshape x11 -> x0, local copies, waits for them, and re-layouts: 6.51 us -> none  [the longest x7 4.81 us: wide(): return vec.astype(F32).reshape(LAYERS, -1, half)]
  transfers between devices with their start and end apart: 1 -> 0, of which waited for: 1 -> 0; matrix products, arithmetic and copies ran while one was open for 2% -> 0% of each run, Pallas kernels for 0% -> 0%
where the time goes in v2:
time: 257 us
  Pallas kernels  256 us (100%)
    pallas_call x1, Pallas kernels, per_device(): pl.pallas_call(functools.partial(step_kernel, (width, cols, units, half),...  252 us

profile of v2, /device:TPU:0, one launch (start us, length us, event | category | flops | bytes accessed | tf_op | source)
XLA Modules:
  0.0 257.2 jit_solution(8260379731809152192)
XLA Ops:
  0.7 251.6 %encoder_step.1 = (bf16[2,64,768]{2,1,0:T(8,128)(2,1)}, bf16[2,64,768]{2,1,0:T(8,128)(2,1)}, bf16[24,192,384]{2,1,0:T(8,128)(2,1)}, f32[2,24,768]{2,1,0:T(8,128)}) custom-call(bf16[2,64,768]{2,1,0:T(8,128)(2,1)} %refs_0_.1, bf16[2,64,768]{2,1,0:T(8,128)(2,1)} %refs_1_.1, s32[2,1024]{1,0:T(2,128)} %refs_2_.1, bf16[2,384]{1,0:T(2,128)(2,1)} %refs_3_.1, ...), custom_call_target="tpu_custom_call" | custom-call | tf_op jit(solution)/shard_map/encoder_step/pallas_call | solution.py:1094
  252.3 4.7 %write_out.1 = (bf16[2,64,768]{2,1,0:T(8,128)(2,1)}, f32[2,64,768]{2,1,0:T(8,128)}, f32[2,192,384]{2,1,0:T(8,128)}, f32[2,192,384]{2,1,0:T(8,128)}, f32[2,192,38...) custom-call(bf16[2,64,768]{2,1,0:T(8,128)(2,1)} %get-tuple-element.3, ...), custom_call_target="tpu_custom_call" | custom-call | tf_op jit(solution)/shard_map/write_out/pallas_call | solution.py:1112

commit v3 on v2

--- a/solution.py
+++ b/solution.py
@@ -15,7 +15,9 @@
 BF16 = jnp.bfloat16
 NEG = -1e30
 VEC_ROWS = 24
+PIECES = 2
 LAGS = (4, 6, 8, 10)
+VEC_TICKS = (1, 2, 5, 7)
 
 
 def nn(a, b):
@@ -143,6 +145,7 @@
     rows = 2 * part
     own_rows = 4 * rows
     all_rows = 8 * rows
+    tall = rows // PIECES
     s = lax.axis_index("shard")
     c = lax.axis_index("ctx")
     t = lax.axis_index("tp")
@@ -406,51 +409,71 @@
     own_ids = jnp.where(hf == 0, ids[:, :own_rows], ids[:, own_rows:])
     IDC[...] = jnp.broadcast_to(own_ids, (128, own_rows)).T
 
+    def piece(ch):
+        return slice(ch * tall, (ch + 1) * tall)
+
     def gather_copies(buf, ssem, rsem):
-        return (
-            rc(buf.at[t], buf.at[t], ssem.at[0], rsem.at[0], c, tc),
-            rc(buf.at[t], buf.at[t], ssem.at[1], rsem.at[1], c, ty),
-            rc(buf.at[ty], buf.at[ty], ssem.at[2], rsem.at[2], c, tc),
-        )
-
-    def gather_start(copies):
-        copies[1].start()
-        copies[0].start()
+        def move(slot, ch, at, tt):
+            view = buf.at[slot, pl.ds(ch * tall, tall)]
+            return rc(view, view, ssem.at[3 * ch + at], rsem.at[3 * ch + at], c, tt)
+
+        return [(move(t, ch, 0, tc), move(t, ch, 1, ty), move(ty, ch, 2, tc)) for ch in range(PIECES)]
+
+    def gather_start(copies, ch):
+        copies[ch][1].start()
+        copies[ch][0].start()
+
+    def gather_near(copies):
+        for to_c, _, _ in copies:
+            to_c.wait_recv()
 
     def gather_remote(copies):
-        copies[1].wait_recv()
-        copies[2].start()
-        copies[2].wait_recv()
+        for _, to_y, y_to_c in copies:
+            to_y.wait_recv()
+            y_to_c.start()
+        for _, _, y_to_c in copies:
+            y_to_c.wait_recv()
 
     def gather_finish(copies):
-        for copy in copies:
-            copy.wait_send()
+        for moves in copies:
+            for copy in moves:
+                copy.wait_send()
 
     def sum_copies(slot, lane):
-        return (
-            rc(SB.at[lane, 0], RB.at[slot, 0], rs_s.at[slot, 0], rs_r.at[slot, 0], c, tc),
-            rc(SB.at[lane, 1], RB.at[slot, 1], rs_s.at[slot, 1], rs_r.at[slot, 1], c, ty),
-            rc(SB.at[lane, 2], RB.at[slot, 2], rs_s.at[slot, 2], rs_r.at[slot, 2], c, tc),
-        )
+        def move(at, ch, tt):
+            where = pl.ds(ch * tall, tall)
+            sem = PIECES * at + ch
+            return rc(SB.at[lane, at, where], RB.at[slot, at, where], rs_s.at[slot, sem], rs_r.at[slot, sem], c, tt)
+
+        pairs = [(move(0, ch, tc), move(1, ch, ty)) for ch in range(PIECES)]
+        last = 2 * PIECES
+        return pairs, rc(SB.at[lane, 2], RB.at[slot, 2], rs_s.at[slot, last], rs_r.at[slot, last], c, tc)
 
     def sum_remote(copies, pf, slot, lane):
-        SB[lane, 0] = pf[(1 - y) * 2 + 1 - k].astype(BF16)
-        copies[0].start()
-        copies[0].wait_recv()
-        SB[lane, 1] = (pf[ty] + RB[slot, 0].astype(F32)).astype(BF16)
-        copies[1].start()
+        for ch, (to_c, _) in enumerate(copies[0]):
+            SB[lane, 0, piece(ch)] = pf[(1 - y) * 2 + 1 - k, piece(ch)].astype(BF16)
+            to_c.start()
+        for ch, (to_c, to_y) in enumerate(copies[0]):
+            to_c.wait_recv()
+            SB[lane, 1, piece(ch)] = (pf[ty, piece(ch)] + RB[slot, 0, piece(ch)].astype(F32)).astype(BF16)
+            to_y.start()
 
     def sum_local(copies, pf, slot, lane):
         SB[lane, 2] = pf[tc].astype(BF16)
-        copies[2].start()
-
-    def sum_finish(copies, pf, slot, lane):
-        copies[2].wait_recv()
-        partial = pf[t] + RB[slot, 2].astype(F32)
-        copies[1].wait_recv()
-        for copy in copies:
-            copy.wait_send()
-        return partial + RB[slot, 1].astype(F32)
+        copies[1].start()
+
+    def sum_finish(copies, pf, slot, lane, ch):
+        pairs, near = copies
+        if ch == 0:
+            near.wait_recv()
+        partial = pf[t, piece(ch)] + RB[slot, 2, piece(ch)].astype(F32)
+        pairs[ch][1].wait_recv()
+        if ch == PIECES - 1:
+            for to_c, to_y in pairs:
+                to_c.wait_send()
+                to_y.wait_send()
+            near.wait_send()
+        return partial + RB[slot, 1, piece(ch)].astype(F32)
 
     def full_vec(layer, row):
         return jnp.concatenate([VB[0, layer, row : row + 1], VB[1, layer, row : row + 1]], axis=1)
@@ -466,7 +489,37 @@
     if fused:
         vec_copy.wait()
     spread_wait(tok_ref, TK, 0)
+    own = hf * 4
+    far = (1 - hf) * 4
+
+    def input_copies(layer):
+        buf = XB.at[layer]
+
+        def move(slot, ch, at, cc, tt):
+            view = buf.at[slot, pl.ds(ch * tall, tall)]
+            return rc(view, view, g8_s.at[layer, 7 * ch + at], g8_r.at[layer, 7 * ch + at], cc, tt)
+
+        return [
+            (
+                move(own + t, ch, 0, c, ty),
+                move(own + t, ch, 1, zp, t),
+                move(own + t, ch, 2, c, tc),
+                move(own + ty, ch, 3, c, tc),
+                move(far + t, ch, 4, c, ty),
+                move(far + t, ch, 5, c, tc),
+                move(far + ty, ch, 6, c, tc),
+            )
+            for ch in range(PIECES)
+        ]
+
+    def input_start(layer, ch):
+        for copy in input_copies(layer)[ch][:3]:
+            copy.start()
+
     H[...] = TK[...].astype(F32)
+    XB[0, own + t] = TK[...]
+    for ch in range(PIECES):
+        input_start(0, ch)
     lane_low = lax.broadcasted_iota(jnp.int32, (1, 2 * HD), 1) < HD
 
     def head_cols(value, head):
@@ -481,21 +534,7 @@
     tile = own_rows // 2
 
     def forward_layer(layer, carry):
-        buf = XB.at[layer]
-        own = hf * 4
-        far = (1 - hf) * 4
-        ss, rr = g8_s.at[layer], g8_r.at[layer]
-        XB[layer, own + t] = H[...].astype(BF16)
-        to_y = rc(buf.at[own + t], buf.at[own + t], ss.at[0], rr.at[0], c, ty)
-        to_z = rc(buf.at[own + t], buf.at[own + t], ss.at[1], rr.at[1], zp, t)
-        to_c = rc(buf.at[own + t], buf.at[own + t], ss.at[2], rr.at[2], c, tc)
-        y_to_c = rc(buf.at[own + ty], buf.at[own + ty], ss.at[3], rr.at[3], c, tc)
-        z_to_y = rc(buf.at[far + t], buf.at[far + t], ss.at[4], rr.at[4], c, ty)
-        z_to_c = rc(buf.at[far + t], buf.at[far + t], ss.at[5], rr.at[5], c, tc)
-        zy_to_c = rc(buf.at[far + ty], buf.at[far + ty], ss.at[6], rr.at[6], c, tc)
-        to_y.start()
-        to_z.start()
-        to_c.start()
+        arrivals = input_copies(layer)
         fetch_wait(layer, (0, 1, 2))
 
         def project(at, with_q):
@@ -509,23 +548,31 @@
             K[layer, where] = nt(block, WQ[layer, cols : 2 * cols]).astype(BF16)
             V[layer, where] = (nt(block, WQ[layer, 2 * cols :]) + vec_at(layer, 2 + k, cols)).astype(BF16)
 
-        to_c.wait_recv()
+        for moves in arrivals:
+            moves[2].wait_recv()
         project(own + 2 * y, True)
-        to_z.wait_recv()
-        z_to_y.start()
-        z_to_c.start()
-        to_y.wait_recv()
-        y_to_c.start()
-        y_to_c.wait_recv()
+        for moves in arrivals:
+            moves[1].wait_recv()
+            moves[4].start()
+            moves[5].start()
+            moves[0].wait_recv()
+            moves[3].start()
+        for moves in arrivals:
+            moves[3].wait_recv()
         project(own + 2 * (1 - y), True)
-        z_to_c.wait_recv()
+        for moves in arrivals:
+            moves[5].wait_recv()
         project(far + 2 * y, False)
-        z_to_y.wait_recv()
-        zy_to_c.start()
-        zy_to_c.wait_recv()
+        for moves in arrivals:
+            moves[4].wait_recv()
+            moves[6].start()
+        for moves in arrivals:
+            moves[6].wait_recv()
         project(far + 2 * (1 - y), False)
-        for copy in (to_y, to_z, to_c, y_to_c, z_to_y, z_to_c, zy_to_c):
-            copy.wait_send()
+        for moves in arrivals:
+            for copy in moves:
+                copy.wait_send()
+        fetch_pass(layer, (4, 5))
 
         def attend(at, inner):
             where = pl.ds(pl.multiple_of(at * tile, tile), tile)
@@ -546,6 +593,7 @@
 
         lax.fori_loop(0, 2, attend, 0)
         fetch_wait(layer, (3,))
+        fetch_pass(layer, (6, 7))
 
         def project_out(at):
             where = pl.ds(pl.multiple_of(at * 2 * rows, 2 * rows), 2 * rows)
@@ -556,17 +604,18 @@
         sum_remote(copies, PF, 0, 0)
         project_out(y)
         sum_local(copies, PF, 0, 0)
-        fetch_pass(layer, (4, 5, 6, 7))
-        branch = sum_finish(copies, PF, 0, 0) + full_vec(layer, 4)
-        normed, xhat, rstd = norm_forward(H[...] + branch, full_vec(layer, 6), full_vec(layer, 7))
-        N1[...] = normed
-        XH1[layer] = xhat
-        SD1[layer] = jnp.broadcast_to(rstd, (rows, 128))
-
-        N1B[layer, t] = normed.astype(BF16)
+        fetch_pass(layer, (8, 9))
         moves = gather_copies(N1B.at[layer], g4_s.at[layer, 0], g4_r.at[layer, 0])
-        gather_start(moves)
-        fetch_pass(layer, (8, 9, 10, 11))
+        for ch in range(PIECES):
+            branch = sum_finish(copies, PF, 0, 0, ch) + full_vec(layer, 4)
+            resid = H[piece(ch)] + branch
+            normed, xhat, rstd = norm_forward(resid, full_vec(layer, 6), full_vec(layer, 7))
+            N1B[layer, t, piece(ch)] = normed.astype(BF16)
+            gather_start(moves, ch)
+            N1[piece(ch)] = normed
+            XH1[layer, piece(ch)] = xhat
+            SD1[layer, piece(ch)] = jnp.broadcast_to(rstd, (tall, 128))
+        fetch_pass(layer, (10, 11))
         fetch_wait(layer, (4, 5, 6, 7))
 
         def feed(at):
@@ -582,32 +631,40 @@
             PF[pl.ds(at * 2, 2)] = nn(low, WU[layer]).reshape(2, rows, width)
 
         copies = sum_copies(1, 0)
-        moves[0].wait_recv()
+        gather_near(moves)
         fetch_wait(layer, (8, 9, 10, 11))
         feed(y)
         sum_local(copies, PF, 1, 0)
+
+        @pl.when(layer == 0)
+        def _():
+            fetch_pass(1, (0, 1, 2, 3))
+
         gather_remote(moves)
         feed(1 - y)
         sum_remote(copies, PF, 1, 0)
         gather_finish(moves)
-
-        @pl.when(layer == 0)
-        def _():
-            fetch_pass(1, (0, 1, 2, 3))
-
-        second = N1[...] + sum_finish(copies, PF, 1, 0) + full_vec(layer, 5)
-        result, xhat, rstd = norm_forward(second, full_vec(layer, 8), full_vec(layer, 9))
-        XH2[layer] = xhat
-        SD2[layer] = jnp.broadcast_to(rstd, (rows, 128))
-        H[...] = result
+        following = jnp.minimum(layer + 1, LAYERS - 1)
+        for ch in range(PIECES):
+            second = N1[piece(ch)] + sum_finish(copies, PF, 1, 0, ch) + full_vec(layer, 5)
+            result, xhat, rstd = norm_forward(second, full_vec(layer, 8), full_vec(layer, 9))
+            low = result.astype(BF16)
+            TK[piece(ch)] = low
+
+            @pl.when(layer + 1 < LAYERS)
+            def _():
+                XB[following, own + t, piece(ch)] = low
+                input_start(following, ch)
+
+            XH2[layer, piece(ch)] = xhat
+            SD2[layer, piece(ch)] = jnp.broadcast_to(rstd, (tall, 128))
+            H[piece(ch)] = result
         return carry
 
     lax.fori_loop(0, LAYERS, forward_layer, 0)
 
-    TK[...] = H[...].astype(BF16)
     collect_start(TK, OT, 2)
     spread_wait(cot_ref, CO, 1)
-    H[...] = CO[...].astype(F32)
 
     total_units = 12 * LAYERS
 
@@ -673,7 +730,7 @@
             def _(stage=stage, unit=unit):
                 stage(unit)
 
-    def vec_step(layer, at):
+    def vec_step(at):
         partner = (
             (s, c, tc),
             (s, c, ty),
@@ -682,21 +739,21 @@
             (s, lax.rem(c + 2, 4), t),
         )[at]
         return pltpu.make_async_remote_copy(
-            src_ref=OV.at[layer],
-            dst_ref=VR.at[layer, at],
-            send_sem=v_s.at[layer, at],
-            recv_sem=v_r.at[layer, at],
+            src_ref=OV,
+            dst_ref=VR.at[at],
+            send_sem=v_s.at[at],
+            recv_sem=v_r.at[at],
             device_id=partner,
             device_id_type=MESH,
         )
 
-    def vec_move(layer, at):
+    def vec_move(at):
         if fused:
             if at > 0:
-                vec_step(layer, at - 1).wait()
-                OV[layer] += VR[layer, at - 1]
+                vec_step(at - 1).wait()
+                OV[...] += VR[at - 1]
             if at < 5:
-                vec_step(layer, at).start()
+                vec_step(at).start()
 
     def side_of(own_side):
         if fused:
@@ -723,6 +780,15 @@
             if not own_side:
                 send_units(base, step, count)
 
+    def across(layer, ch):
+        where = pl.ds(ch * tall, tall)
+        return rc(ZS.at[where], ZR.at[layer, where], rz_s.at[layer, ch], rz_r.at[layer, ch], zp, t)
+
+    def layer_grad(layer, ch):
+        near = sum_finish(sum_copies(4, 0), PF.at[pl.ds(own, 4)], 4, 0, ch)
+        across(layer, ch).wait()
+        return DR1[piece(ch)] + near + ZR[layer, piece(ch)].astype(F32)
+
     def backward_layer(turn, carry):
         layer = LAYERS - 1 - turn
         base = turn * 12
@@ -732,21 +798,25 @@
                 for i in places:
                     advance(base + i)
 
-        def late_vec(at):
+        moves = gather_copies(DF, g4_s.at[layer, 1], g4_r.at[layer, 1])
+        above = jnp.minimum(layer + 1, LAYERS - 1)
+        for ch in range(PIECES):
+
+            @pl.when(turn == 0)
+            def _():
+                H[piece(ch)] = CO[piece(ch)].astype(F32)
+
             @pl.when(turn > 0)
             def _():
-                vec_move(LAYERS - 1, at)
-
-        grad = H[...]
-        xhat = XH2[layer]
-        rstd = SD2[layer][:, :1]
-        d_second = norm_backward(grad, xhat, rstd, full_vec(layer, 8))
-        put_vec(layer, 4, jnp.sum(grad * xhat, axis=0, keepdims=True))
-        put_vec(layer, 5, jnp.sum(grad, axis=0, keepdims=True))
-        DR[...] = d_second
-        DF[t] = d_second.astype(BF16)
-        moves = gather_copies(DF, g4_s.at[layer, 1], g4_r.at[layer, 1])
-        gather_start(moves)
+                H[piece(ch)] = layer_grad(above, ch)
+
+            rstd = SD2[layer, piece(ch)][:, :1]
+            d_second = norm_backward(H[piece(ch)], XH2[layer, piece(ch)], rstd, full_vec(layer, 8))
+            DF[t, piece(ch)] = d_second.astype(BF16)
+            gather_start(moves, ch)
+            DR[piece(ch)] = d_second
+        put_vec(layer, 4, jnp.sum(H[...] * XH2[layer], axis=0, keepdims=True))
+        put_vec(layer, 5, jnp.sum(H[...], axis=0, keepdims=True))
         copies = sum_copies(2, 0)
 
         def back_feed(at):
@@ -757,11 +827,10 @@
             DU[where] = low
             PF[pl.ds(at * 2, 2)] = nt(low, WI[layer]).reshape(2, rows, width)
 
-        moves[0].wait_recv()
+        gather_near(moves)
         back_feed(y)
         sum_local(copies, PF, 2, 0)
         tick(0, 1)
-        late_vec(0)
         gather_remote(moves)
         back_feed(1 - y)
         sum_remote(copies, PF, 2, 0)
@@ -779,30 +848,30 @@
             if not own_side:
                 send_units(base, 4, 4)
         tick(3)
-        late_vec(1)
         only = jnp.where(t == 0, 1.0, 0.0)
         put_vec(layer, 0, only * jnp.sum(DF[...].reshape(own_rows, width).astype(F32), axis=0, keepdims=True))
         put_vec(layer, 14 + t, jnp.sum(DU[...].astype(F32), axis=0, keepdims=True))
 
-        d_normed = DR[...] + sum_finish(copies, PF, 2, 0)
-        xhat = XH1[layer]
-        d_first = norm_backward(d_normed, xhat, SD1[layer][:, :1], full_vec(layer, 6))
-        put_vec(layer, 2, jnp.sum(d_normed * xhat, axis=0, keepdims=True))
-        put_vec(layer, 3, jnp.sum(d_normed, axis=0, keepdims=True))
-        DR1[...] = d_first
-        DA[t] = d_first.astype(BF16)
         moves = gather_copies(DA, g4_s.at[layer, 2], g4_r.at[layer, 2])
-        gather_start(moves)
+        for ch in range(PIECES):
+            d_normed = DR[piece(ch)] + sum_finish(copies, PF, 2, 0, ch)
+            rstd = SD1[layer, piece(ch)][:, :1]
+            d_first = norm_backward(d_normed, XH1[layer, piece(ch)], rstd, full_vec(layer, 6))
+            DA[t, piece(ch)] = d_first.astype(BF16)
+            gather_start(moves, ch)
+            DR1[piece(ch)] = d_first
+            DR[piece(ch)] = d_normed
+        put_vec(layer, 2, jnp.sum(DR[...] * XH1[layer], axis=0, keepdims=True))
+        put_vec(layer, 3, jnp.sum(DR[...], axis=0, keepdims=True))
 
         def back_out(at):
             where = pl.ds(pl.multiple_of(at * 2 * rows, 2 * rows), 2 * rows)
             block = DA[pl.ds(at * 2, 2)].reshape(2 * rows, width)
             DOB[where] = nt(block, WO[layer]).astype(BF16)
 
-        moves[0].wait_recv()
+        gather_near(moves)
         back_out(y)
         tick(4, 5)
-        late_vec(2)
         gather_remote(moves)
         back_out(1 - y)
         gather_finish(moves)
@@ -835,12 +904,9 @@
 
         tick(6)
         lax.fori_loop(0, 2, back_attend, 0)
-        tick(7, 8)
-        late_vec(3)
+        tick(7)
         DK[...] = DKF[...].astype(BF16)
         DV[...] = DVF[...].astype(BF16)
-        own = hf * 4
-        far = (1 - hf) * 4
 
         def back_in(at, with_q):
             where = pl.ds(pl.multiple_of(at * rows, 2 * rows), 2 * rows)
@@ -862,11 +928,10 @@
         sum_remote(copies, pf_own, 4, 0)
         back_in(own + 2 * y, True)
         sum_local(copies, pf_own, 4, 0)
-        ZS[...] = sum_finish(far_copies, pf_far, 3, 1).astype(BF16)
-        across = rc(ZS, ZR.at[layer], rz_s.at[layer], rz_r.at[layer], zp, t)
-        across.start()
-        tick(9)
-        late_vec(4)
+        for ch in range(PIECES):
+            ZS[piece(ch)] = sum_finish(far_copies, pf_far, 3, 1, ch).astype(BF16)
+            across(layer, ch).start()
+        tick(8, 9)
 
         def block_cols(ref, start, count):
             return lambda at: ref[pl.ds(start, count), :, pl.ds(at, half)].reshape(-1, half)
@@ -879,25 +944,21 @@
         put_vec(layer, 6 + t, jnp.sum(DQ[...].astype(F32), axis=0, keepdims=True))
         put_vec(layer, 10 + t, jnp.sum(DV[...].astype(F32), axis=0, keepdims=True))
 
-        near = sum_finish(copies, pf_own, 4, 0)
         tick(11)
-        late_vec(5)
-        across.wait()
-        H[...] = DR1[...] + near + ZR[layer].astype(F32)
         return carry
 
     lax.fori_loop(0, LAYERS, backward_layer, 0)
-    CO[...] = H[...].astype(BF16)
+    for ch in range(PIECES):
+        CO[piece(ch)] = layer_grad(0, ch).astype(BF16)
     collect_start(CO, OG, 3)
-    vec_move(0, 0)
+    vec_move(0)
     if fused:
         more = LAGS[3]
-        spots = [0, more // 5, 2 * more // 5, 3 * more // 5, 4 * more // 5]
         for i in range(more):
-            if i in spots[1:]:
-                vec_move(0, spots.index(i))
+            if i in VEC_TICKS:
+                vec_move(1 + VEC_TICKS.index(i))
             advance(total_units + i)
-        vec_move(0, 5)
+        vec_move(5)
 
         def drain(i, carry):
             pltpu.make_async_copy(GO.at[i], out_mat.at[i], om_sem.at[i]).wait()
@@ -1061,24 +1122,24 @@
         vm((n_units, cols, half), BF16),
         vm((n_units, cols, half), BF16),
         vm((LAYERS, VEC_ROWS, width), F32),
-        vm((LAYERS, 5, VEC_ROWS, width), F32),
+        vm((5, LAYERS, VEC_ROWS, width), F32),
         dma((LAYERS, 6)),
         dma((LAYERS, 13)),
         dma((LAYERS, 13)),
         dma((LAYERS, 12)),
         dma((LAYERS, 12)),
-        dma((LAYERS, 5)),
-        dma((LAYERS, 5)),
+        dma((5,)),
+        dma((5,)),
         dma((4, 2)),
         dma((4, 2)),
-        dma((LAYERS, 7)),
-        dma((LAYERS, 7)),
-        dma((LAYERS, 3, 3)),
-        dma((LAYERS, 3, 3)),
-        dma((5, 3)),
-        dma((5, 3)),
-        dma((LAYERS,)),
-        dma((LAYERS,)),
+        dma((LAYERS, 7 * PIECES)),
+        dma((LAYERS, 7 * PIECES)),
+        dma((LAYERS, 3, 3 * PIECES)),
+        dma((LAYERS, 3, 3 * PIECES)),
+        dma((5, 2 * PIECES + 1)),
+        dma((5, 2 * PIECES + 1)),
+        dma((LAYERS, PIECES)),
+        dma((LAYERS, PIECES)),
         dma((n_units,)),
         dma((n_units,)),
         dma((n_units,)),

time: 257 us -> 238 us (0.926)
  Pallas kernels: 256 us -> 237 us
    pallas_call x1, Pallas kernels: 252 us -> 233 us  [per_device(): pl.pallas_call(functools.partial(step_kernel, (width, cols, units, half),...]
where the time goes in v3:
time: 238 us
  Pallas kernels  237 us (100%)
    pallas_call x1, Pallas kernels, per_device(): pl.pallas_call(functools.partial(step_kernel, (width, cols, units, half),...  233 us

profile of v3, /device:TPU:0, one launch (start us, length us, event | category | flops | bytes accessed | tf_op | source)
XLA Modules:
  0.0 238.3 jit_solution(7821201144472395412)
XLA Ops:
  0.7 232.7 %encoder_step.1 = (bf16[2,64,768]{2,1,0:T(8,128)(2,1)}, bf16[2,64,768]{2,1,0:T(8,128)(2,1)}, bf16[24,192,384]{2,1,0:T(8,128)(2,1)}, f32[2,24,768]{2,1,0:T(8,128)}) custom-call(bf16[2,64,768]{2,1,0:T(8,128)(2,1)} %refs_0_.1, bf16[2,64,768]{2,1,0:T(8,128)(2,1)} %refs_1_.1, s32[2,1024]{1,0:T(2,128)} %refs_2_.1, bf16[2,384]{1,0:T(2,128)(2,1)} %refs_3_.1, ...), custom_call_target="tpu_custom_call" | custom-call | tf_op jit(solution)/shard_map/encoder_step/pallas_call | solution.py:1155
  233.4 4.7 %write_out.1 = (bf16[2,64,768]{2,1,0:T(8,128)(2,1)}, f32[2,64,768]{2,1,0:T(8,128)}, f32[2,192,384]{2,1,0:T(8,128)}, f32[2,192,384]{2,1,0:T(8,128)}, f32[2,192,38...) custom-call(bf16[2,64,768]{2,1,0:T(8,128)(2,1)} %get-tuple-element.3, ...), custom_call_target="tpu_custom_call" | custom-call | tf_op jit(solution)/shard_map/write_out/pallas_call | solution.py:1173

commit v4 on v3

--- a/solution.py
+++ b/solution.py
@@ -14,10 +14,11 @@
 F32 = jnp.float32
 BF16 = jnp.bfloat16
 NEG = -1e30
-VEC_ROWS = 24
-PIECES = 2
+VEC_ROWS = 32
+PIECES = 4
+RING = 8
 LAGS = (4, 6, 8, 10)
-VEC_TICKS = (1, 2, 5, 7)
+VEC_TICKS = (0, 1, 4, 6, 8, 9)
 
 
 def nn(a, b):
@@ -113,6 +114,8 @@
         Y2,
         OV,
         VR,
+        VQ,
+        OW,
         wl_sem,
         ws_sem,
         wr_sem,
@@ -183,7 +186,6 @@
                 )
     if fused:
         pl.semaphore_signal(bar, 1, device_id=(1 - s, c, t), device_id_type=MESH)
-    pl.semaphore_wait(bar, 16 if fused else 15)
 
     def unit_view(layer, item, side):
         at = pl.multiple_of(side * half, half)
@@ -219,8 +221,8 @@
         return rc(
             unit_arg(layer, item),
             unit_view(layer, item, s),
-            ws_sem.at[layer, item],
-            wr_sem.at[layer, item],
+            ws_sem.at[layer, item if item < 4 else 2 + item // 2],
+            wr_sem.at[layer, item if item < 4 else 2 + item // 2],
             c,
             t,
             1 - s,
@@ -228,7 +230,7 @@
 
     def over_z(layer, item):
         view = unit_view(layer, item, 1 - s)
-        return rc(view, view, wz_s.at[layer, item], wz_r.at[layer, item], zp, t)
+        return rc(view, view, wz_s.at[layer, item // 2], wz_r.at[layer, item // 2], zp, t)
 
     def direct(layer, item):
         return jnp.logical_and(layer == 0, item < 4)
@@ -286,15 +288,24 @@
             for j in range(4):
                 VB[side, layer, 10 + j : 11 + j] = value[:, j * half : (j + 1) * half]
 
+    for layer in range(LAYERS):
+        for item in range(6):
+            local_copy(layer, item).start()
     if fused:
         fill_vectors(s, 0)
-        vec_copy = rc(VB.at[s], VB.at[s], ws_sem.at[0, 12], wr_sem.at[0, 12], c, t, 1 - s)
-        vec_copy.start()
     else:
         fill_vectors(0, 0)
         fill_vectors(1, half)
-
     b_me = c // 2
+    ids = seg_ref[pl.ds(b_me, 1)]
+    places = lax.broadcasted_iota(jnp.int32, ids.shape, 1)
+    ids = jnp.where(places < len_ref[b_me], ids, -1).astype(F32)
+    IDR[...] = jnp.broadcast_to(ids, IDR.shape)
+    own_ids = jnp.where(hf == 0, ids[:, :own_rows], ids[:, own_rows:])
+    IDC[...] = jnp.broadcast_to(own_ids, (128, own_rows)).T
+    OV[...] = jnp.zeros_like(OV)
+    pl.semaphore_wait(bar, 16 if fused else 15)
+
     spread_t = 2 * hf + y
 
     def spread_copies(src_ref, dst_ref, which):
@@ -394,28 +405,21 @@
                 ).wait_recv()
 
     spread_start(tok_ref, TK, 0)
-    for layer in range(LAYERS):
-        if fused:
+    if fused:
+        vec_copy = rc(VB.at[s], VB.at[s], ws_sem.at[0, 8], wr_sem.at[0, 8], c, t, 1 - s)
+        vec_copy.start()
+        for layer in range(LAYERS):
             for item in range(12):
                 fetch_start(layer, item)
-        for item in range(6):
-            local_copy(layer, item).start()
     spread_start(cot_ref, CO, 1)
-
-    ids = seg_ref[pl.ds(b_me, 1)]
-    places = lax.broadcasted_iota(jnp.int32, ids.shape, 1)
-    ids = jnp.where(places < len_ref[b_me], ids, -1).astype(F32)
-    IDR[...] = jnp.broadcast_to(ids, IDR.shape)
-    own_ids = jnp.where(hf == 0, ids[:, :own_rows], ids[:, own_rows:])
-    IDC[...] = jnp.broadcast_to(own_ids, (128, own_rows)).T
 
     def piece(ch):
         return slice(ch * tall, (ch + 1) * tall)
 
-    def gather_copies(buf, ssem, rsem):
+    def gather_copies(buf):
         def move(slot, ch, at, tt):
             view = buf.at[slot, pl.ds(ch * tall, tall)]
-            return rc(view, view, ssem.at[3 * ch + at], rsem.at[3 * ch + at], c, tt)
+            return rc(view, view, g4_s.at[3 * ch + at], g4_r.at[3 * ch + at], c, tt)
 
         return [(move(t, ch, 0, tc), move(t, ch, 1, ty), move(ty, ch, 2, tc)) for ch in range(PIECES)]
 
@@ -443,11 +447,11 @@
         def move(at, ch, tt):
             where = pl.ds(ch * tall, tall)
             sem = PIECES * at + ch
-            return rc(SB.at[lane, at, where], RB.at[slot, at, where], rs_s.at[slot, sem], rs_r.at[slot, sem], c, tt)
+            return rc(SB.at[lane, at, where], RB.at[slot, at, where], rs_s.at[lane, sem], rs_r.at[lane, sem], c, tt)
 
         pairs = [(move(0, ch, tc), move(1, ch, ty)) for ch in range(PIECES)]
         last = 2 * PIECES
-        return pairs, rc(SB.at[lane, 2], RB.at[slot, 2], rs_s.at[slot, last], rs_r.at[slot, last], c, tc)
+        return pairs, rc(SB.at[lane, 2], RB.at[slot, 2], rs_s.at[lane, last], rs_r.at[lane, last], c, tc)
 
     def sum_remote(copies, pf, slot, lane):
         for ch, (to_c, _) in enumerate(copies[0]):
@@ -480,8 +484,6 @@
 
     def vec_at(layer, row, lanes):
         return VB[y, layer, pl.ds(row, 1)][:, :lanes]
-
-    OV[...] = jnp.zeros_like(OV)
 
     def put_vec(layer, row, value):
         OV[layer, pl.ds(row, 1), : value.shape[1]] = value
@@ -605,7 +607,7 @@
         project_out(y)
         sum_local(copies, PF, 0, 0)
         fetch_pass(layer, (8, 9))
-        moves = gather_copies(N1B.at[layer], g4_s.at[layer, 0], g4_r.at[layer, 0])
+        moves = gather_copies(N1B.at[layer])
         for ch in range(PIECES):
             branch = sum_finish(copies, PF, 0, 0, ch) + full_vec(layer, 4)
             resid = H[piece(ch)] + branch
@@ -663,22 +665,21 @@
 
     lax.fori_loop(0, LAYERS, forward_layer, 0)
 
-    collect_start(TK, OT, 2)
     spread_wait(cot_ref, CO, 1)
 
     total_units = 12 * LAYERS
 
     def x_copy(unit):
-        return rc(GS.at[lax.rem(unit, 12)], XR.at[unit], xs_s.at[unit], xs_r.at[unit], c, t, 1 - s)
+        return rc(GS.at[lax.rem(unit, 12)], XR.at[unit], xs_s.at[lax.rem(unit, 12)], xs_r.at[unit], c, t, 1 - s)
 
     def z1_copy(unit):
-        return rc(GO.at[unit], YR.at[unit], z1_s.at[unit], z1_r.at[unit], z_in, t)
+        return rc(GO.at[unit], YR.at[unit], z1_s.at[lax.rem(unit, RING)], z1_r.at[lax.rem(unit, RING)], z_in, t)
 
     def z2_copy(unit):
-        return rc(GO.at[unit], Y2.at[unit], z2_s.at[unit], z2_r.at[unit], z_mid, t)
+        return rc(GO.at[unit], Y2.at[unit], z2_s.at[lax.rem(unit, RING)], z2_r.at[lax.rem(unit, RING)], z_mid, t)
 
     def z3_copy(unit):
-        return rc(GO.at[unit], YR.at[unit], z3_s.at[unit], z3_r.at[unit], z_out, t)
+        return rc(GO.at[unit], YR.at[unit], z3_s.at[lax.rem(unit, RING)], z3_r.at[lax.rem(unit, RING)], z_out, t)
 
     def add_into(unit, other):
         GO[unit] = (GO[unit].astype(F32) + other.astype(F32)).astype(BF16)
@@ -709,16 +710,23 @@
             add_into(unit, Y2[unit])
             z3_copy(unit).start()
 
+    def out_copy(src, unit):
+        return pltpu.make_async_copy(src.at[unit], out_mat.at[unit], om_sem.at[lax.rem(unit, RING)])
+
     def stage_out(unit):
+        @pl.when(unit >= RING)
+        def _():
+            out_copy(GO, unit - RING).wait()
+
         @pl.when(is_inner)
         def _():
             z3_copy(unit).wait_send()
-            pltpu.make_async_copy(GO.at[unit], out_mat.at[unit], om_sem.at[unit]).start()
+            out_copy(GO, unit).start()
 
         @pl.when(is_outer)
         def _():
             z3_copy(unit).wait_recv()
-            pltpu.make_async_copy(YR.at[unit], out_mat.at[unit], om_sem.at[unit]).start()
+            out_copy(YR, unit).start()
 
     stages = ((stage_out, LAGS[3]), (stage_z3, LAGS[2]), (stage_z2, LAGS[1]), (stage_z1, LAGS[0]))
 
@@ -737,22 +745,41 @@
             (1 - s, c, t),
             (s, zp, t),
             (s, lax.rem(c + 2, 4), t),
+            (s, c, tc),
+            (s, c, ty),
         )[at]
+        if at < 2:
+            src, dst = OV, VR.at[at]
+        elif at < 5:
+            src, dst = OW.at[:, vec_rows(t)], VQ.at[at - 2]
+        elif at == 5:
+            src = dst = OW.at[:, vec_rows(t)]
+        else:
+            src = dst = OW.at[:, pl.ds(pl.multiple_of(y * (VEC_ROWS // 2), VEC_ROWS // 2), VEC_ROWS // 2)]
         return pltpu.make_async_remote_copy(
-            src_ref=OV,
-            dst_ref=VR.at[at],
+            src_ref=src,
+            dst_ref=dst,
             send_sem=v_s.at[at],
             recv_sem=v_r.at[at],
             device_id=partner,
             device_id_type=MESH,
         )
 
+    def vec_rows(place):
+        count = VEC_ROWS // 4
+        return pl.ds(pl.multiple_of(place * count, count), count)
+
     def vec_move(at):
         if fused:
             if at > 0:
                 vec_step(at - 1).wait()
-                OV[...] += VR[at - 1]
-            if at < 5:
+                if at == 1:
+                    OV[...] += VR[0]
+                elif at == 2:
+                    OW[:, vec_rows(t)] = OV[:, vec_rows(t)] + VR[1, :, vec_rows(t)]
+                elif at <= 5:
+                    OW[:, vec_rows(t)] += VQ[at - 3]
+            if at < 7:
                 vec_step(at).start()
 
     def side_of(own_side):
@@ -798,7 +825,7 @@
                 for i in places:
                     advance(base + i)
 
-        moves = gather_copies(DF, g4_s.at[layer, 1], g4_r.at[layer, 1])
+        moves = gather_copies(DF)
         above = jnp.minimum(layer + 1, LAYERS - 1)
         for ch in range(PIECES):
 
@@ -815,6 +842,11 @@
             DF[t, piece(ch)] = d_second.astype(BF16)
             gather_start(moves, ch)
             DR[piece(ch)] = d_second
+
+        @pl.when(turn == 0)
+        def _():
+            collect_start(TK, OT, 2)
+
         put_vec(layer, 4, jnp.sum(H[...] * XH2[layer], axis=0, keepdims=True))
         put_vec(layer, 5, jnp.sum(H[...], axis=0, keepdims=True))
         copies = sum_copies(2, 0)
@@ -852,7 +884,7 @@
         put_vec(layer, 0, only * jnp.sum(DF[...].reshape(own_rows, width).astype(F32), axis=0, keepdims=True))
         put_vec(layer, 14 + t, jnp.sum(DU[...].astype(F32), axis=0, keepdims=True))
 
-        moves = gather_copies(DA, g4_s.at[layer, 2], g4_r.at[layer, 2])
+        moves = gather_copies(DA)
         for ch in range(PIECES):
             d_normed = DR[piece(ch)] + sum_finish(copies, PF, 2, 0, ch)
             rstd = SD1[layer, piece(ch)][:, :1]
@@ -958,13 +990,13 @@
             if i in VEC_TICKS:
                 vec_move(1 + VEC_TICKS.index(i))
             advance(total_units + i)
-        vec_move(5)
+        vec_move(7)
 
         def drain(i, carry):
-            pltpu.make_async_copy(GO.at[i], out_mat.at[i], om_sem.at[i]).wait()
+            out_copy(GO, i).wait()
             return carry
 
-        lax.fori_loop(0, total_units, drain, 0)
+        lax.fori_loop(total_units - RING, total_units, drain, 0)
         for layer in range(LAYERS):
             fetch_drain(layer)
     else:
@@ -974,7 +1006,7 @@
         far_out.start()
         own_out.wait()
         far_out.wait()
-    out_vec[...] = OV[...]
+    out_vec[...] = (OW if fused else OV)[...]
     collect_wait(TK, OT, 2)
     out_tok[...] = OT[...]
     collect_wait(CO, OG, 3)
@@ -1122,33 +1154,35 @@
         vm((n_units, cols, half), BF16),
         vm((n_units, cols, half), BF16),
         vm((LAYERS, VEC_ROWS, width), F32),
-        vm((5, LAYERS, VEC_ROWS, width), F32),
+        vm((2, LAYERS, VEC_ROWS, width), F32),
+        vm((3, LAYERS, VEC_ROWS // 4, width), F32),
+        vm((LAYERS, VEC_ROWS, width), F32),
         dma((LAYERS, 6)),
-        dma((LAYERS, 13)),
-        dma((LAYERS, 13)),
-        dma((LAYERS, 12)),
-        dma((LAYERS, 12)),
-        dma((5,)),
-        dma((5,)),
+        dma((LAYERS, 9)),
+        dma((LAYERS, 9)),
+        dma((LAYERS, 6)),
+        dma((LAYERS, 6)),
+        dma((7,)),
+        dma((7,)),
         dma((4, 2)),
         dma((4, 2)),
         dma((LAYERS, 7 * PIECES)),
         dma((LAYERS, 7 * PIECES)),
-        dma((LAYERS, 3, 3 * PIECES)),
-        dma((LAYERS, 3, 3 * PIECES)),
-        dma((5, 2 * PIECES + 1)),
-        dma((5, 2 * PIECES + 1)),
+        dma((3 * PIECES,)),
+        dma((3 * PIECES,)),
+        dma((2, 2 * PIECES + 1)),
+        dma((2, 2 * PIECES + 1)),
         dma((LAYERS, PIECES)),
         dma((LAYERS, PIECES)),
+        dma((12,)),
         dma((n_units,)),
-        dma((n_units,)),
-        dma((n_units,)),
-        dma((n_units,)),
-        dma((n_units,)),
-        dma((n_units,)),
-        dma((n_units,)),
-        dma((n_units,)),
-        dma((n_units,)),
+        dma((RING,)),
+        dma((RING,)),
+        dma((RING,)),
+        dma((RING,)),
+        dma((RING,)),
+        dma((RING,)),
+        dma((RING,)),
     ]
     vmem = pl.BlockSpec(memory_space=pltpu.VMEM)
     hbm = pl.BlockSpec(memory_space=pl.ANY)

time: 238 us -> 230 us (0.966)
  Pallas kernels: 237 us -> 229 us
    pallas_call x1, Pallas kernels: 233 us -> 224 us  [per_device(): pl.pallas_call(functools.partial(step_kernel, (width, cols, units, half),...]
where the time goes in v4:
time: 230 us
  Pallas kernels  229 us (100%)
    pallas_call x1, Pallas kernels, per_device(): pl.pallas_call(functools.partial(step_kernel, (width, cols, units, half),...  224 us
    pallas_call x1, Pallas kernels, per_device(): pl.pallas_call(functools.partial(finish_kernel, dims), grid=(LAYERS,), ou...  4.76 us

profile of v4, /device:TPU:0, one launch (start us, length us, event | category | flops | bytes accessed | tf_op | source)
XLA Modules:
  0.0 230.1 jit_solution(17280812904777421443)
XLA Ops:
  0.7 224.5 %encoder_step.1 = (bf16[2,64,768]{2,1,0:T(8,128)(2,1)}, bf16[2,64,768]{2,1,0:T(8,128)(2,1)}, bf16[24,192,384]{2,1,0:T(8,128)(2,1)}, f32[2,32,768]{2,1,0:T(8,128)}) custom-call(bf16[2,64,768]{2,1,0:T(8,128)(2,1)} %refs_0_.1, bf16[2,64,768]{2,1,0:T(8,128)(2,1)} %refs_1_.1, s32[2,1024]{1,0:T(2,128)} %refs_2_.1, bf16[2,384]{1,0:T(2,128)(2,1)} %refs_3_.1, ...), custom_call_target="tpu_custom_call" | custom-call | tf_op jit(solution)/shard_map/encoder_step/pallas_call | solution.py:1189
  225.2 4.8 %write_out.1 = (bf16[2,64,768]{2,1,0:T(8,128)(2,1)}, f32[2,64,768]{2,1,0:T(8,128)}, f32[2,192,384]{2,1,0:T(8,128)}, f32[2,192,384]{2,1,0:T(8,128)}, f32[2,192,38...) custom-call(bf16[2,64,768]{2,1,0:T(8,128)(2,1)} %get-tuple-element.3, ...), custom_call_target="tpu_custom_call" | custom-call | tf_op jit(solution)/shard_map/write_out/pallas_call | solution.py:1207

commit v5 on v4

--- a/solution.py
+++ b/solution.py
@@ -18,7 +18,7 @@
 PIECES = 4
 RING = 8
 LAGS = (4, 6, 8, 10)
-VEC_TICKS = (0, 1, 4, 6, 8, 9)
+VEC_TICKS = (0, 1, 3, 5, 6, 8)
 
 
 def nn(a, b):
@@ -936,7 +936,7 @@
 
         tick(6)
         lax.fori_loop(0, 2, back_attend, 0)
-        tick(7)
+        tick(7, 8)
         DK[...] = DKF[...].astype(BF16)
         DV[...] = DVF[...].astype(BF16)
 
@@ -963,7 +963,7 @@
         for ch in range(PIECES):
             ZS[piece(ch)] = sum_finish(far_copies, pf_far, 3, 1, ch).astype(BF16)
             across(layer, ch).start()
-        tick(8, 9)
+        tick(9)
 
         def block_cols(ref, start, count):
             return lambda at: ref[pl.ds(start, count), :, pl.ds(at, half)].reshape(-1, half)

time: 230 us -> 229 us (level)
  no operation moved by 1% of the time
where the time goes in v5:
time: 229 us
  Pallas kernels  228 us (100%)
    pallas_call x1, Pallas kernels, per_device(): pl.pallas_call(functools.partial(step_kernel, (width, cols, units, half),...  223 us
    pallas_call x1, Pallas kernels, per_device(): pl.pallas_call(functools.partial(finish_kernel, dims), grid=(LAYERS,), ou...  4.76 us

profile of v5, /device:TPU:0, one launch (start us, length us, event | category | flops | bytes accessed | tf_op | source)
XLA Modules:
  0.0 229.0 jit_solution(16135012860171890373)
XLA Ops:
  0.7 223.4 %encoder_step.1 = (bf16[2,64,768]{2,1,0:T(8,128)(2,1)}, bf16[2,64,768]{2,1,0:T(8,128)(2,1)}, bf16[24,192,384]{2,1,0:T(8,128)(2,1)}, f32[2,32,768]{2,1,0:T(8,128)}) custom-call(bf16[2,64,768]{2,1,0:T(8,128)(2,1)} %refs_0_.1, bf16[2,64,768]{2,1,0:T(8,128)(2,1)} %refs_1_.1, s32[2,1024]{1,0:T(2,128)} %refs_2_.1, bf16[2,384]{1,0:T(2,128)(2,1)} %refs_3_.1, ...), custom_call_target="tpu_custom_call" | custom-call | tf_op jit(solution)/shard_map/encoder_step/pallas_call | solution.py:1189
  224.0 4.8 %write_out.1 = (bf16[2,64,768]{2,1,0:T(8,128)(2,1)}, f32[2,64,768]{2,1,0:T(8,128)}, f32[2,192,384]{2,1,0:T(8,128)}, f32[2,192,384]{2,1,0:T(8,128)}, f32[2,192,38...) custom-call(bf16[2,64,768]{2,1,0:T(8,128)(2,1)} %get-tuple-element.3, ...), custom_call_target="tpu_custom_call" | custom-call | tf_op jit(solution)/shard_map/write_out/pallas_call | solution.py:1207
